TPU v7x, 32 devices: a whole 2x2x4 slice. The times are simulated.
32 devices in a mesh: grp: 2 (over y), ctx: 4 (over x, core), head: 4 (over z).
Axes of the slice: x: 2, y: 2, z: 4, core: 2. Of those that a mesh axis runs over, the one named last changes fastest.
Arguments:
- prompt_hidden: bfloat16 [4, 1024, 4096], P('grp', 'ctx', 'head'), parts along dimension 0, may hold values from -3 to 3
- qkv_weight: bfloat16 [3, 4096, 4096], P(None, 'ctx', 'head'), may hold values from -0.09375 to 0.09375
- out_weight: bfloat16 [4096, 4096], P('head', 'ctx'), may hold values from -0.9375 to 0.9375
- embed_table: bfloat16 [32768, 4096], P('ctx', 'head'), may hold values from -60 to 60
- response_ids: int32 [4, 256], P(None, 'grp'), parts along dimension 1, may hold values from 0 to 32767
- assignment: int32 [256], P('grp'), parts along dimension 0, may hold values from 0 to 1
Outputs:
- final_hidden: bfloat16 [4, 256, 4096], P(None, ('grp', 'ctx'), 'head'), parts along dimension 1
There are 2 independent parts, one for each index of `grp`. A program takes and returns all parts, laid end to end along the dimension named above; an argument that names none is the same for every part. Nothing has to cross between parts.
All inputs are finite; a program needn't handle non-finite values.
Results may differ from a plain program's by a relative error of at most 0.023.
Values may be sent and summed in bfloat16 or wider, within the bound.
A program may use at most 128 MiB of HBM per device.

v0:
```python
import jax
import jax.numpy as jnp
from jax import lax
from jax.sharding import PartitionSpec as P

DH = 128


def rms_rows(values):
    return values * lax.rsqrt(jnp.mean(values * values, axis=-1, keepdims=True) + 1e-06)


def on_device(prompt_hidden, qkv_weight, out_weight, embed_table, response_ids, assignment):
    local_cols = prompt_hidden.shape[2]
    prompt_rows = prompt_hidden.shape[1]
    head_size = DH
    local_heads = local_cols // head_size
    steps = response_ids.shape[0]
    resp_local = response_ids.shape[1] // lax.axis_size("ctx")
    ctx_index = lax.axis_index("ctx")
    full_rows = lax.all_gather(qkv_weight, "ctx", axis=1, tiled=True)
    kv_weight = jnp.concatenate([full_rows[1], full_rows[2]], axis=1)
    piece = lax.all_gather(prompt_hidden, "head", axis=2, tiled=True)
    flat_piece = piece.reshape(2 * prompt_rows, piece.shape[2])
    kv_local = jnp.dot(flat_piece, kv_weight, preferred_element_type=jnp.float32)
    kv_local = kv_local.astype(jnp.bfloat16).reshape(2, prompt_rows, 2, local_heads, head_size)
    partial_state = jnp.einsum(
        "pthd,pthe->phde", kv_local[:, :, 0], kv_local[:, :, 1], preferred_element_type=jnp.float32
    )
    state = lax.psum(partial_state.astype(jnp.bfloat16), "ctx").astype(jnp.float32)
    vocab_rows = embed_table.shape[0]
    offset_ids = response_ids - ctx_index * vocab_rows
    inside = (offset_ids >= 0) & (offset_ids < vocab_rows)
    looked = jnp.take(embed_table, jnp.clip(offset_ids, 0, vocab_rows - 1), axis=0)
    looked = jnp.where(inside[:, :, None], looked.astype(jnp.float32), 0.0)
    embedded_mine = lax.psum_scatter(
        looked.astype(jnp.bfloat16), "ctx", scatter_dimension=1, tiled=True
    )
    embedded = lax.all_gather(embedded_mine, "head", axis=2, tiled=True)
    normed = rms_rows(embedded.astype(jnp.float32)).astype(jnp.bfloat16)
    projected_qkv = jnp.einsum(
        "trd,kde->trke", normed, full_rows, preferred_element_type=jnp.float32
    ).astype(jnp.bfloat16)
    projected_qkv = projected_qkv.reshape(steps, resp_local, 3, local_heads, head_size)
    query = projected_qkv[:, :, 0]
    key = projected_qkv[:, :, 1]
    value = projected_qkv[:, :, 2]
    my_prompt = lax.dynamic_slice_in_dim(assignment, ctx_index * resp_local, resp_local, 0)
    query_f = query.astype(jnp.float32)
    both = jnp.einsum("trhd,phde->ptrhe", query_f, state, precision=lax.Precision.HIGHEST)
    chosen = jnp.where((my_prompt == 0)[None, :, None, None], both[0], both[1])
    scores = jnp.einsum("trhd,srhd->rhts", query, key, preferred_element_type=jnp.float32)
    later = jnp.arange(steps)[:, None] >= jnp.arange(steps)[None, :]
    scores = jnp.where(later[None, None], scores, 0.0).astype(jnp.bfloat16)
    local = jnp.einsum("rhts,srhd->trhd", scores, value, preferred_element_type=jnp.float32)
    head_out = rms_rows(chosen + local).astype(jnp.bfloat16).reshape(steps, resp_local, local_cols)
    terms = jnp.einsum(
        "trd,de->tre",
        head_out,
        lax.all_gather(out_weight, "ctx", axis=1, tiled=True),
        preferred_element_type=jnp.float32,
    )
    width = terms.shape[2]
    mine = lax.psum_scatter(
        terms.astype(jnp.bfloat16), "head", scatter_dimension=2, tiled=True
    ).astype(jnp.float32)
    mixed = embedded_mine.astype(jnp.float32) + mine
    squares = lax.psum(jnp.sum(mixed * mixed, axis=-1), "head")
    result = mixed * lax.rsqrt(squares[:, :, None] / width + 1e-06)
    return result.astype(jnp.bfloat16)


def solution(mesh):
    return jax.shard_map(
        on_device,
        mesh=mesh,
        in_specs=(
            P("grp", "ctx", "head"),
            P(None, "ctx", "head"),
            P("head", "ctx"),
            P("ctx", "head"),
            P(None, "grp"),
            P("grp"),
        ),
        out_specs=P(None, ("grp", "ctx"), "head"),
        check_vma=False,
    )
```

profile of v0, /device:TPU:0, one launch (start us, length us, event | category | flops | bytes accessed | tf_op | source)
XLA Modules:
  0.0 461.3 jit_solution(4606842393122182999)
XLA Ops:
  6.5 0.7 compare_and_fusion.1
  7.9 10.7 %gather_fusion = bf16[512,1024]{1,0:T(8,128)(2,1)S(1)} fusion(bf16[8192,1024]{1,0:T(8,128)(2,1)} %param.9, s32[1024]{0:T(1024)S(1)} %pad_clamp_fusion), kind=kCustom, calls=%fused_computation | custom fusion | bytes 2099200 | tf_op jit(solution)/shard_map/jit(_take)/gather | solution.py:34
  18.6 1.4 select_convert_fusion
  20.0 0.7 all-gather.5.cloned.1.call-update
  21.5 26.1 %reduce-scatter.3.cloned.1.call-done = bf16[4,32,1024]{2,1,0:T(8,128)(2,1)} async-done(((bf16[4,128,1024]{2,1,0:T(8,128)(2,1)}), bf16[4,32,1024]{2,1,0:T(8,128)(2,1)}) %reduce-scatter.3.cloned.1.call-update) | async-done | bytes 262160 | tf_op jit(solution)/shard_map/reduce_scatter | solution.py:36
  47.9 156.1 %all-gather.5.cloned.1.call-done = bf16[3,4096,1024]{2,1,0:T(8,128)(2,1)} async-done(((bf16[3,1024,1024]{2,1,0:T(8,128)(2,1)}), bf16[3,4096,1024]{2,1,0:T(8,128)(2,1)}) %all-gather.5.cloned.1.call-update) | async-done | bytes 25165840 | tf_op jit(solution)/shard_map/all_gather | solution.py:21
  204.0 11.8 %slice_bitcast_fusion.1 = (bf16[4096,1024]{1,0:T(8,128)(2,1)}, bf16[4096,1024]{1,0:T(8,128)(2,1)}) fusion(bf16[3,4096,1024]{2,1,0:T(8,128)(2,1)} %all-gather.5.cloned.1.call-done), kind=kLoop, calls=%fused_computation.8 | loop fusion | bytes 33554432 | tf_op jit(solution)/shard_map/squeeze | solution.py:22
  215.9 70.5 %all-gather.7.cloned.1.call-done = bf16[2,256,4096]{2,1,0:T(8,128)(2,1)} async-done(((bf16[2,256,1024]{2,1,0:T(8,128)(2,1)}), bf16[2,256,4096]{2,1,0:T(8,128)(2,1)}) %all-gather.7.cloned.1.call-update) | async-done | bytes 4194320 | tf_op jit(solution)/shard_map/all_gather | solution.py:23
  286.4 17.3 %fusion.14 = bf16[512,2048]{0,1:T(8,128)(2,1)} fusion(bf16[512,4096]{1,0:T(8,128)(2,1)} %bitcast.86, bf16[4096,1024]{1,0:T(8,128)(2,1)} %get-tuple-element.8, bf16[4096,1024]{1,0:T(8,128)(2,1)} %get-tuple-element.7), kind=kOutput, calls=%fused_computation.13 | convolution fusion | flops 8624537600 | bytes 23068672 | tf_op jit(solution)/shard_map/dot_general | solution.py:25
  303.7 2.6 reshape.52
  306.3 1.5 slice_bitcast_fusion.3
  307.8 1.3 convolution_convert_fusion
  310.0 4.3 all-gather.9.cloned.1.call-done
  314.3 1.5 fusion.17
  315.9 12.1 %fusion.19 = bf16[4,32,3,1024]{3,1,2,0:T(8,128)(2,1)S(1)} fusion(bf16[3,4096,1024]{2,1,0:T(8,128)(2,1)} %all-gather.5.cloned.1.call-done, bf16[4,32,4096]{2,1,0:T(8,128)(2,1)} %all-gather.9.cloned.1.call-done, f32[4,32]{1,0:T(4,128)S(1)} %add_rsqrt_fusion.2), kind=kOutput, calls=%fused_computation.19 | convolution fusion | flops 3223191552 | bytes 27001344 | tf_op jit(solution)/shard_map/trd,kde->trke/dot_general | solution.py:41
  328.3 0.7 fusion.23
  329.0 20.3 %all-reduce.2.cloned.1.call-done = bf16[2,8,128,128]{3,2,0,1:T(8,128)(2,1)} async-done(((bf16[2,8,128,128]{3,2,0,1:T(8,128)(2,1)}), bf16[2,8,128,128]{3,2,0,1:T(8,128)(2,1)}) %all-reduce.2.cloned.1.call-update) | async-done | bytes 524304 | tf_op jit(solution)/shard_map/psum | solution.py:30
  349.3 1.3 convolution_bitcast_fusion
  351.1 58.0 %all-gather.11.cloned.1.call-done = bf16[1024,4096]{1,0:T(8,128)(2,1)} async-done(((bf16[1024,1024]{1,0:T(8,128)(2,1)}), bf16[1024,4096]{1,0:T(8,128)(2,1)}) %all-gather.11.cloned.1.call-update) | async-done | bytes 8388624 | tf_op jit(solution)/shard_map/all_gather | solution.py:60
  409.2 5.7 %fusion.8 = bf16[4,32,4096]{2,1,0:T(8,128)(2,1)} fusion(bf16[1024,4096]{1,0:T(8,128)(2,1)} %all-gather.11.cloned.1.call-done, f32[4,32,8,128]{3,1,0,2:T(8,128)S(1)} %get-tuple-element.6, f32[4,32,8]{1,0,2:T(4,128)S(1)} %add_rsqrt_fusion), kind=kOutput, calls=%fused_computation.11 | convolution fusion | flops 1074528256 | bytes 9965568 | tf_op jit(solution)/shard_map/trd,de->tre/dot_general | solution.py:57
  414.9 27.4 %reduce-scatter.5.cloned.1.call-done = bf16[4,32,1024]{2,1,0:T(8,128)(2,1)} async-done(((bf16[4,32,4096]{2,1,0:T(8,128)(2,1)}), bf16[4,32,1024]{2,1,0:T(8,128)(2,1)}) %reduce-scatter.5.cloned.1.call-update) | async-done | bytes 262160 | tf_op jit(solution)/shard_map/reduce_scatter | solution.py:64
  442.3 1.1 multiply_reduce_fusion
  443.4 9.3 %psum.15 = f32[4,32]{1,0:T(4,128)S(1)} all-reduce(f32[4,32]{1,0:T(4,128)S(1)} %multiply_reduce_fusion), channel_id=1, replica_groups=mesh['grp'=2,'ctx'=4,'head'=4] {'head'}, use_global_device_ids=true, to_apply=%region_6.7 | all-reduce | flops 128 | bytes 1024 | tf_op jit(solution)/shard_map/psum | solution.py:68
  452.7 1.8 multiply_convert_fusion
  (27 shorter events, 3.5 us)
Async XLA Ops:
  6.5 41.1 %reduce-scatter.3.cloned.1.call-start = ((), (), s32[]{:S(2)}) async-start(), calls=%async_computation.2 | async-start | bytes 1310720 | tf_op jit(solution)/shard_map/reduce_scatter | solution.py:36
  20.0 184.1 %all-gather.5.cloned.1.call-start = ((), (), s32[]{:S(2)}) async-start(), calls=%async_computation.3 | async-start | bytes 31457280 | tf_op jit(solution)/shard_map/all_gather | solution.py:21
  20.7 265.7 %all-gather.7.cloned.1.call-start = ((), (), s32[]{:S(2)}) async-start(), calls=%async_computation.4 | async-start | bytes 5242880 | tf_op jit(solution)/shard_map/all_gather | solution.py:23
  21.5 292.8 %all-gather.9.cloned.1.call-start = ((), (), s32[]{:S(2)}) async-start(), calls=%async_computation.6 | async-start | bytes 1310720 | tf_op jit(solution)/shard_map/all_gather | solution.py:39
  47.7 301.7 %all-reduce.2.cloned.1.call-start = ((), (), s32[]{:S(2)}) async-start(), calls=%async_computation.5 | async-start | bytes 1048576 | tf_op jit(solution)/shard_map/psum | solution.py:30
  303.7 6.2 %copy-start.1 = (s32[128]{0:T(128)S(1)}, s32[128]{0:T(128)}, u32[]{:S(2)}) copy-start(s32[128]{0:T(128)} %param.11) | copy-start | bytes 1540
  309.1 100.1 %all-gather.11.cloned.1.call-start = ((), (), s32[]{:S(2)}) async-start(), calls=%async_computation.7 | async-start | bytes 10485760 | tf_op jit(solution)/shard_map/all_gather | solution.py:60
  309.7 132.6 %reduce-scatter.5.cloned.1.call-start = ((), (), s32[]{:S(2)}) async-start(), calls=%async_computation.8 | async-start | bytes 1310720 | tf_op jit(solution)/shard_map/reduce_scatter | solution.py:64
  329.0 113.3 %copy-start = (bf16[4,32,1024]{2,1,0:T(8,128)(2,1)S(1)}, bf16[4,32,1024]{2,1,0:T(8,128)(2,1)}, u32[]{:S(2)}) copy-start(bf16[4,32,1024]{2,1,0:T(8,128)(2,1)} %reduce-scatter.3.cloned.1.call-done) | copy-start | bytes 786436
Sparse Core Ops, SparseCore 0:
  20.1 27.4 reduce-scatter.2
  49.2 154.7 all-gather.4
  205.6 80.7 all-gather.6
  287.8 26.4 all-gather.8
  316.5 32.7 all-reduce.1
  350.8 58.3 all-gather.10
  415.0 27.2 reduce-scatter.4
where the time goes:
time: 462 us; the launch traced here: 461 us
  waiting for transfers between devices  365 us (79%)
  matrix products  38.4 us (8%)
  local copies, waits for them, and re-layouts  26.9 us (6%)
  between operations  13.6 us (3%)
  blocking collectives  9.28 us (2%)
  other arithmetic  7.7 us (2%)
    all_gather x1, waiting for transfers between devices, on_device(): full_rows = lax.all_gather(qkv_weight, 'ctx', axis=1, tiled=True)  156 us
    all_gather x1, waiting for transfers between devices, on_device(): piece = lax.all_gather(prompt_hidden, 'head', axis=2, tiled=True)  70.5 us
    all_gather x1, waiting for transfers between devices, on_device(): lax.all_gather(out_weight, 'ctx', axis=1, tiled=True)  58 us
    reduce_scatter x1, waiting for transfers between devices, on_device(): lax.psum_scatter(terms.astype(jnp.bfloat16), 'head', scatter_dimension=2,...  27.4 us
    reduce_scatter x1, waiting for transfers between devices, on_device(): lax.psum_scatter(looked.astype(jnp.bfloat16), 'ctx', scatter_dimension=1,...  26.1 us
    psum x1, waiting for transfers between devices, on_device(): lax.psum(partial_state.astype(jnp.bfloat16), 'ctx').astype(jnp.float32)  20.3 us
    dot_general x1, matrix products, on_device(): jnp.dot(flat_piece, kv_weight, preferred_element_type=jnp.float32)  17.3 us
    dot_general x1, matrix products, on_device(): jnp.einsum('trd,kde->trke', normed, full_rows, preferred_element_type=jnp...  12.1 us
  transfers between devices with their start and end apart: 7, of which 7 were waited for; matrix products, arithmetic and copies ran while one was open for 11% of the time, Pallas kernels for 0%

commit v1 on v0

v1 whole, which is shorter than its diff:
```python
import functools

import jax
import jax.numpy as jnp
from jax import lax
from jax.experimental import pallas as pl
from jax.experimental.pallas import tpu as pltpu
from jax.sharding import PartitionSpec as P

DH = 128
SUB = 2
MESH = pl.DeviceIdType.MESH


def rms_rows(values):
    return values * lax.rsqrt(jnp.mean(values * values, axis=-1, keepdims=True) + 1e-06)


def remote(src, dst, send, recv, target):
    return pltpu.make_async_remote_copy(
        src_ref=src, dst_ref=dst, send_sem=send, recv_sem=recv,
        device_id=target, device_id_type=MESH,
    )


def greet(axes):
    barrier = pltpu.get_barrier_semaphore()
    total = 0
    for axis, size in axes:
        me = lax.axis_index(axis)
        for step in range(1, size):
            pl.semaphore_signal(
                barrier, inc=1, device_id={axis: lax.rem(me + step, size)}, device_id_type=MESH
            )
        total += size - 1
    pl.semaphore_wait(barrier, total)


def gather_kernel(sizes, p_ref, w_ref, o_ref, looked_ref, pf_ref, wf_ref, of_ref, ef_ref, em_ref,
                  e_in, own_sem, e_send, e_recv, z_send, z_recv, x_send, x_recv,
                  y_send, y_recv, pown_send, pown_recv, px_send, px_recv, py_send, py_recv):
    grp_n, ctx_n, head_n = sizes
    chips = ctx_n // 2
    grp, ctx, head = lax.axis_index("grp"), lax.axis_index("ctx"), lax.axis_index("head")
    chip, core = ctx // 2, lax.rem(ctx, 2)
    partner = {"ctx": chip * 2 + 1 - core}
    kinds, rows, cols = w_ref.shape
    o_rows, o_cols = o_ref.shape
    width = p_ref.shape[2]
    resp = em_ref.shape[1]
    w_sub = rows // (grp_n * SUB)
    o_sub = o_rows // (grp_n * SUB)
    chunks = [(kind, sub) for kind in (1, 2, 0, 3) for sub in range(SUB)]

    def chunk_dst(index, shard, part):
        kind, sub = chunks[index]
        if kind == 3:
            start = pl.multiple_of((part * SUB + sub) * o_sub, o_sub)
            return of_ref.at[pl.ds(start, o_sub), pl.ds(pl.multiple_of(shard * o_cols, o_cols), o_cols)]
        start = pl.multiple_of(shard * rows + (part * SUB + sub) * w_sub, w_sub)
        return wf_ref.at[kind, pl.ds(start, w_sub), :]

    def chunk_src(index, part):
        kind, sub = chunks[index]
        if kind == 3:
            return o_ref.at[pl.ds(pl.multiple_of((part * SUB + sub) * o_sub, o_sub), o_sub), :]
        return w_ref.at[kind, pl.ds(pl.multiple_of((part * SUB + sub) * w_sub, w_sub), w_sub), :]

    def prompt_at(owner):
        return pf_ref.at[:, :, pl.ds(pl.multiple_of(owner * width, width), width)]

    def embed_at(owner):
        return ef_ref.at[:, :, pl.ds(pl.multiple_of(owner * width, width), width)]

    def w_at(shard):
        return wf_ref.at[:, pl.ds(pl.multiple_of(shard * rows, rows), rows), :]

    def o_at(shard):
        return of_ref.at[:, pl.ds(pl.multiple_of(shard * o_cols, o_cols), o_cols)]

    greet((("grp", grp_n), ("ctx", ctx_n), ("head", head_n)))

    ends = []

    def at_end(ok, fn):
        ends.append((ok, fn))

    for step in range(1, ctx_n):
        to = lax.rem(ctx + step, ctx_n)
        copy = remote(
            looked_ref.at[:, pl.ds(pl.multiple_of(to * resp, resp), resp), :], e_in.at[step - 1],
            e_send.at[step - 1], e_recv.at[step - 1], {"ctx": to},
        )
        copy.start()
        at_end(None, copy.wait_send)

    def x_copy(src, index, way, dist, shard):
        return remote(src, chunk_dst(index, shard, grp), x_send.at[way, dist - 1, index],
                      x_recv.at[way, dist - 1, index], {"ctx": ctx + (2 if way == 0 else -2)})

    def z_copy(src, dst, what, way, dist):
        return remote(src, dst, z_send.at[what, way, dist - 1], z_recv.at[what, way, dist - 1],
                      {"head": head + (1 if way == 0 else -1)})

    x_next = (chip + 1 < chips, chip > 0)
    z_next = (head + 1 < head_n, head > 0)

    def start_if(ok, copy):
        pl.when(ok)(copy.start)
        at_end(ok, copy.wait_send)

    for way in range(2):
        start_if(z_next[way], z_copy(p_ref, prompt_at(head), 0, way, 1))
    for index in range(len(chunks)):
        for way in range(2):
            if chips > 1:
                start_if(x_next[way], x_copy(chunk_src(index, grp), index, way, 1, ctx))

    mate = chip * 2 + 1 - core
    for number, (src, dst) in enumerate(((w_ref, w_at), (o_ref, o_at))):
        local = pltpu.make_async_copy(src, dst(ctx), own_sem.at[number])
        local.start()
        at_end(None, local.wait)
        copy = remote(src, dst(ctx), pown_send.at[number], pown_recv.at[number], partner)
        copy.start()
        at_end(None, copy.wait_send)
        at_end(None, remote(src, dst(mate), pown_send.at[number], pown_recv.at[number], partner).wait_recv)
    local = pltpu.make_async_copy(p_ref, prompt_at(head), own_sem.at[2])
    local.start()
    at_end(None, local.wait)

    total = looked_ref[:, pl.ds(pl.multiple_of(ctx * resp, resp), resp), :].astype(jnp.float32)
    for step in range(1, ctx_n):
        remote(e_in.at[step - 1], e_in.at[step - 1], e_send.at[step - 1], e_recv.at[step - 1], partner).wait_recv()
        total += e_in[step - 1].astype(jnp.float32)
    em_ref[...] = total.astype(em_ref.dtype)
    local = pltpu.make_async_copy(em_ref, embed_at(head), own_sem.at[3])
    local.start()
    at_end(None, local.wait)
    for way in range(2):
        start_if(z_next[way], z_copy(em_ref, embed_at(head), 1, way, 1))

    events = []

    def z_event(what, way, dist):
        owner = head - dist if way == 0 else head + dist
        have = owner >= 0 if way == 0 else owner < head_n
        place = (prompt_at, embed_at)[what](owner)

        @pl.when(have)
        def _():
            z_copy(place, place, what, way, dist).wait_recv()

        if dist + 1 < head_n:
            ok = have & z_next[way]
            start_if(ok, z_copy(place, place, what, way, dist + 1))

    for dist in range(1, head_n):
        for way in range(2):
            events.append((22.0 * dist, functools.partial(z_event, 0, way, dist)))
            events.append((22.0 * dist + 5.0, functools.partial(z_event, 1, way, dist)))

    def pass_on(ok, dst, send, recv):
        copy = remote(dst, dst, send, recv, partner)
        start_if(ok, copy)

    def mate_wait(ok, dst, send, recv):
        at_end(ok, remote(dst, dst, send, recv, partner).wait_recv)

    def x_event(index, way, dist):
        from_chip = chip - dist if way == 0 else chip + dist
        have = from_chip >= 0 if way == 0 else from_chip < chips
        place = chunk_dst(index, from_chip * 2 + core, grp)

        @pl.when(have)
        def _():
            x_copy(place, index, way, dist, from_chip * 2 + core).wait_recv()

        if dist + 1 < chips:
            start_if(have & x_next[way], x_copy(place, index, way, dist + 1, from_chip * 2 + core))
        for step in range(1, grp_n):
            start_if(have, remote(place, place, y_send.at[way, dist - 1, step - 1, index],
                                  y_recv.at[way, dist - 1, step - 1, index],
                                  {"grp": lax.rem(grp + step, grp_n)}))
        sems = px_send.at[way, dist - 1, index], px_recv.at[way, dist - 1, index]
        pass_on(have, place, *sems)
        mate_wait(have, chunk_dst(index, from_chip * 2 + 1 - core, grp), *sems)

    def y_event(index, way, dist, step):
        from_chip = chip - dist if way == 0 else chip + dist
        have = from_chip >= 0 if way == 0 else from_chip < chips
        part = lax.rem(grp + grp_n - step, grp_n)
        place = chunk_dst(index, from_chip * 2 + core, part)
        key = (way, dist - 1, step - 1, index)

        @pl.when(have)
        def _():
            remote(place, place, y_send.at[key], y_recv.at[key], partner).wait_recv()

        sems = py_send.at[key], py_recv.at[key]
        pass_on(have, place, *sems)
        mate_wait(have, chunk_dst(index, from_chip * 2 + 1 - core, part), *sems)

    for dist in range(1, chips):
        for index in range(len(chunks)):
            when = 11.0 * (index + 1) + 88.0 * (dist - 1)
            for way in range(2):
                events.append((when, functools.partial(x_event, index, way, dist)))
                for step in range(1, grp_n):
                    events.append((when + 12.0, functools.partial(y_event, index, way, dist, step)))
    for _, fn in sorted(events, key=lambda event: event[0]):
        fn()
    for ok, fn in ends:
        if ok is None:
            fn()
        else:
            pl.when(ok)(fn)


def gather_all(sizes, prompt_hidden, qkv_weight, out_weight, looked):
    grp_n, ctx_n, head_n = sizes
    chips = ctx_n // 2
    kinds, rows, cols = qkv_weight.shape
    steps, resp_all, width = looked.shape
    resp = resp_all // ctx_n
    n_chunks = (kinds + 1) * SUB
    dtype = prompt_hidden.dtype
    vmem = pl.BlockSpec(memory_space=pltpu.VMEM)
    hbm = pl.BlockSpec(memory_space=pl.ANY)
    far = max(chips - 1, 1)
    x_sem = pltpu.SemaphoreType.DMA((2, far, n_chunks))
    y_sem = pltpu.SemaphoreType.DMA((2, far, max(grp_n - 1, 1), n_chunks))
    z_sem = pltpu.SemaphoreType.DMA((2, 2, max(head_n - 1, 1)))
    return pl.pallas_call(
        functools.partial(gather_kernel, sizes),
        out_shape=(
            jax.ShapeDtypeStruct(prompt_hidden.shape[:2] + (width * head_n,), dtype),
            jax.ShapeDtypeStruct((kinds, rows * ctx_n, cols), dtype),
            jax.ShapeDtypeStruct((out_weight.shape[0], out_weight.shape[1] * ctx_n), dtype),
            jax.ShapeDtypeStruct((steps, resp, width * head_n), dtype),
            jax.ShapeDtypeStruct((steps, resp, width), dtype),
        ),
        in_specs=[vmem] * 4,
        out_specs=(hbm, hbm, hbm, hbm, vmem),
        scratch_shapes=[
            pltpu.VMEM((ctx_n - 1, steps, resp, width), dtype),
            pltpu.SemaphoreType.DMA((4,)),
            pltpu.SemaphoreType.DMA((ctx_n - 1,)),
            pltpu.SemaphoreType.DMA((ctx_n - 1,)),
            z_sem, z_sem, x_sem, x_sem, y_sem, y_sem,
            pltpu.SemaphoreType.DMA((2,)), pltpu.SemaphoreType.DMA((2,)),
            x_sem, x_sem, y_sem, y_sem,
        ],
        compiler_params=pltpu.CompilerParams(collective_id=0, has_side_effects=True),
    )(prompt_hidden, qkv_weight, out_weight, looked)


def on_device(sizes, prompt_hidden, qkv_weight, out_weight, embed_table, response_ids, assignment):
    local_cols = prompt_hidden.shape[2]
    prompt_rows = prompt_hidden.shape[1]
    head_size = DH
    local_heads = local_cols // head_size
    steps = response_ids.shape[0]
    resp_local = response_ids.shape[1] // lax.axis_size("ctx")
    ctx_index = lax.axis_index("ctx")
    vocab_rows = embed_table.shape[0]
    offset_ids = response_ids - ctx_index * vocab_rows
    inside = (offset_ids >= 0) & (offset_ids < vocab_rows)
    looked = jnp.take(embed_table, jnp.clip(offset_ids, 0, vocab_rows - 1), axis=0)
    looked = jnp.where(inside[:, :, None], looked, jnp.zeros((), looked.dtype))
    piece, full_rows, full_out, embedded, embedded_mine = gather_all(
        sizes, prompt_hidden, qkv_weight, out_weight, looked
    )
    flat_piece = piece.reshape(2 * prompt_rows, piece.shape[2])
    keys = jnp.dot(flat_piece, full_rows[1], preferred_element_type=jnp.float32)
    keys = keys.astype(jnp.bfloat16).reshape(2, prompt_rows, local_heads, head_size)
    values = jnp.dot(flat_piece, full_rows[2], preferred_element_type=jnp.float32)
    values = values.astype(jnp.bfloat16).reshape(2, prompt_rows, local_heads, head_size)
    partial_state = jnp.einsum(
        "pthd,pthe->phde", keys, values, preferred_element_type=jnp.float32
    )
    state = lax.psum(partial_state.astype(jnp.bfloat16), "ctx").astype(jnp.float32)
    normed = rms_rows(embedded.astype(jnp.float32)).astype(jnp.bfloat16)
    projected_qkv = jnp.einsum(
        "trd,kde->trke", normed, full_rows, preferred_element_type=jnp.float32
    ).astype(jnp.bfloat16)
    projected_qkv = projected_qkv.reshape(steps, resp_local, 3, local_heads, head_size)
    query = projected_qkv[:, :, 0]
    key = projected_qkv[:, :, 1]
    value = projected_qkv[:, :, 2]
    my_prompt = lax.dynamic_slice_in_dim(assignment, ctx_index * resp_local, resp_local, 0)
    query_f = query.astype(jnp.float32)
    both = jnp.einsum("trhd,phde->ptrhe", query_f, state, precision=lax.Precision.HIGHEST)
    chosen = jnp.where((my_prompt == 0)[None, :, None, None], both[0], both[1])
    scores = jnp.einsum("trhd,srhd->rhts", query, key, preferred_element_type=jnp.float32)
    later = jnp.arange(steps)[:, None] >= jnp.arange(steps)[None, :]
    scores = jnp.where(later[None, None], scores, 0.0).astype(jnp.bfloat16)
    local = jnp.einsum("rhts,srhd->trhd", scores, value, preferred_element_type=jnp.float32)
    head_out = rms_rows(chosen + local).astype(jnp.bfloat16).reshape(steps, resp_local, local_cols)
    terms = jnp.einsum("trd,de->tre", head_out, full_out, preferred_element_type=jnp.float32)
    width = terms.shape[2]
    mine = lax.psum_scatter(
        terms.astype(jnp.bfloat16), "head", scatter_dimension=2, tiled=True
    ).astype(jnp.float32)
    mixed = embedded_mine.astype(jnp.float32) + mine
    squares = lax.psum(jnp.sum(mixed * mixed, axis=-1), "head")
    result = mixed * lax.rsqrt(squares[:, :, None] / width + 1e-06)
    return result.astype(jnp.bfloat16)


def solution(mesh):
    sizes = (mesh.shape["grp"], mesh.shape["ctx"], mesh.shape["head"])
    return jax.shard_map(
        functools.partial(on_device, sizes),
        mesh=mesh,
        in_specs=(
            P("grp", "ctx", "head"),
            P(None, "ctx", "head"),
            P("head", "ctx"),
            P("ctx", "head"),
            P(None, "grp"),
            P("grp"),
        ),
        out_specs=P(None, ("grp", "ctx"), "head"),
        check_vma=False,
    )
```

time: 462 us -> 256 us (0.55)
  waiting for transfers between devices: 365 us -> 46 us
  Pallas kernels: 0 us -> 129 us
  local copies, waits for them, and re-layouts: 26.9 us -> 14.2 us
    all_gather x4 -> x0, waiting for transfers between devices: 289 us -> none  [the longest x1 156 us: on_device(): full_rows = lax.all_gather(qkv_weight, 'ctx', axis=1, tiled=True)]
    pallas_call x0 -> x1, Pallas kernels: none -> 129 us  [gather_all(): pl.pallas_call(functools.partial(gather_kernel, sizes), out_shape=(jax.Sh...]
    reduce_scatter x1 -> x0, waiting for transfers between devices: 26.1 us -> none  [on_device(): lax.psum_scatter(looked.astype(jnp.bfloat16), 'ctx', scatter_dimension=1,...]
    squeeze x2 -> x0, local copies, waits for them, and re-layouts: 13.3 us -> none  [the longest x1 11.8 us: on_device(): kv_weight = jnp.concatenate([full_rows[1], full_rows[2]], axis=1)]
    dot_general x3 -> x4, matrix products: 24.3 us -> 23.3 us  [the longest x1 9.28 us: on_device(): jnp.dot(flat_piece, full_rows[2], preferred_element_type=jnp.float32)]
  transfers between devices with their start and end apart: 7 -> 2, of which waited for: 7 -> 2; matrix products, arithmetic and copies ran while one was open for 11% -> 5% of each run, Pallas kernels for 0% -> 0%
where the time goes in v1:
time: 256 us
  Pallas kernels  129 us (50%)
  waiting for transfers between devices  46 us (18%)
  matrix products  37.1 us (14%)
  local copies, waits for them, and re-layouts  14.2 us (6%)
  between operations  13.5 us (5%)
  blocking collectives  9.28 us (4%)
  other arithmetic  6.31 us (2%)
    pallas_call x1, Pallas kernels, gather_all(): pl.pallas_call(functools.partial(gather_kernel, sizes), out_shape=(jax.Sh...  129 us
    reduce_scatter x1, waiting for transfers between devices, on_device(): lax.psum_scatter(terms.astype(jnp.bfloat16), 'head', scatter_dimension=2,...  27.6 us
    psum x1, waiting for transfers between devices, on_device(): lax.psum(partial_state.astype(jnp.bfloat16), 'ctx').astype(jnp.float32)  18.4 us
    dot_general x1, matrix products, on_device(): jnp.einsum('trd,kde->trke', normed, full_rows, preferred_element_type=jnp...  11.8 us
    gather x1, local copies, waits for them, and re-layouts, on_device(): jnp.take(embed_table, jnp.clip(offset_ids, 0, vocab_rows - 1), axis=0)  10.8 us
    psum x1, blocking collectives, on_device(): squares = lax.psum(jnp.sum(mixed * mixed, axis=-1), 'head')  9.28 us
    dot_general x1, matrix products, on_device(): jnp.dot(flat_piece, full_rows[2], preferred_element_type=jnp.float32)  9.28 us
    dot_general x1, matrix products, on_device(): keys = jnp.dot(flat_piece, full_rows[1], preferred_element_type=jnp.float32)  6.87 us
  transfers between devices with their start and end apart: 2, of which 2 were waited for; matrix products, arithmetic and copies ran while one was open for 5% of the time, Pallas kernels for 0%

profile of v1, /device:TPU:0, one launch (start us, length us, event | category | flops | bytes accessed | tf_op | source)
XLA Modules:
  0.0 255.8 jit_solution(11758231651860763150)
XLA Ops:
  6.5 0.7 compare_and_fusion.1
  7.2 0.7 fusion.49
  7.9 10.8 %gather_fusion = bf16[512,1024]{1,0:T(8,128)(2,1)S(1)} fusion(bf16[8192,1024]{1,0:T(8,128)(2,1)} %param.9, s32[1024]{0:T(1024)S(1)} %pad_clamp_fusion), kind=kCustom, calls=%fused_computation | custom fusion | bytes 2099200 | tf_op jit(solution)/shard_map/jit(_take)/gather | solution.py:269
  18.8 1.2 select_select_fusion.looked_ref
  20.0 129.1 %shard_map.64 = (bf16[2,256,4096]{2,1,0:T(8,128)(2,1)}, bf16[3,4096,1024]{2,1,0:T(8,128)(2,1)}, bf16[1024,4096]{1,0:T(8,128)(2,1)}, bf16[4,32,4096]{2,1,0:T(8,128)(2,1)}, bf16[4,32,1024]{2,1,0:T(8,128)(2,1)}) custom-call(bf16[2,256,1024]{2,1,0:T(8,128)(2,1)} %p_ref.1, bf16[3,1024,1024]{2,1,0:T(8,128)(2,1)} %w_ref.1, bf16[1024,1024]{1,0:T(8,128)(2,1)} %o_ref.1, ...), custom_call_target="tpu_custom_call" | custom-call | tf_op jit(solution)/shard_map/pallas_call | solution.py:234
  149.1 9.3 %fusion.24 = bf16[64,8,8,128]{3,1,2,0:T(8,128)(2,1)S(1)} fusion(bf16[512,4096]{1,0:T(8,128)(2,1)} %bitcast.99, bf16[3,4096,1024]{2,1,0:T(8,128)(2,1)} %get-tuple-element.12), kind=kOutput, calls=%fused_computation.19 | convolution fusion | flops 4295491584 | bytes 13631488 | tf_op jit(solution)/shard_map/dot_general | solution.py:277
  158.4 2.5 copy-done
  160.9 6.9 %fusion.27 = bf16[64,8,8,128]{3,1,2,0:T(8,128)(2,1)S(1)} fusion(bf16[512,4096]{1,0:T(8,128)(2,1)} %bitcast.100, bf16[3,4096,1024]{2,1,0:T(8,128)(2,1)S(1)} %copy-done), kind=kOutput, calls=%fused_computation.20 | convolution fusion | flops 4295491584 | bytes 13631488 | tf_op jit(solution)/shard_map/dot_general | solution.py:275
  167.7 0.3 copy.28
  168.0 0.3 copy.29
  168.3 1.4 convolution_convert_fusion
  169.8 0.3 reduce-scatter.2.cloned.1.call-start
  170.1 0.3 fusion.13
  170.4 11.8 %fusion.21 = bf16[4,32,3,1024]{3,1,2,0:T(8,128)(2,1)S(1)} fusion(bf16[3,4096,1024]{2,1,0:T(8,128)(2,1)} %get-tuple-element.12, bf16[4,32,4096]{2,1,0:T(8,128)(2,1)S(1)} %copy-done.1, f32[4,32]{1,0:T(4,128)S(1)} %add_rsqrt_fusion.2), kind=kOutput, calls=%fused_computation.18 | convolution fusion | flops 3223191552 | bytes 27001344 | tf_op jit(solution)/shard_map/trd,kde->trke/dot_general | solution.py:284
  182.1 0.2 copy.30
  182.5 0.8 fusion.31
  183.3 18.4 %all-reduce.2.cloned.1.call-done = bf16[2,8,128,128]{3,2,0,1:T(8,128)(2,1)} async-done(((bf16[2,8,128,128]{3,2,0,1:T(8,128)(2,1)}), bf16[2,8,128,128]{3,2,0,1:T(8,128)(2,1)}) %all-reduce.2.cloned.1.call-update) | async-done | bytes 524304 | tf_op jit(solution)/shard_map/psum | solution.py:282
  201.7 1.3 convolution_bitcast_fusion
  203.0 0.5 multiply_reduce_fusion.1
  203.5 5.7 %fusion.10 = bf16[4,32,4096]{2,1,0:T(8,128)(2,1)} fusion(bf16[1024,4096]{1,0:T(8,128)(2,1)} %get-tuple-element.14, f32[4,32,8,128]{3,1,0,2:T(8,128)S(1)} %get-tuple-element.16, f32[4,32,8]{1,0,2:T(4,128)S(1)} %add_rsqrt_fusion), kind=kOutput, calls=%fused_computation.11 | convolution fusion | flops 1074528256 | bytes 9965568 | tf_op jit(solution)/shard_map/trd,de->tre/dot_general | solution.py:300
  209.2 27.6 %reduce-scatter.2.cloned.1.call-done = bf16[4,32,1024]{2,1,0:T(8,128)(2,1)} async-done(((bf16[4,32,4096]{2,1,0:T(8,128)(2,1)}), bf16[4,32,1024]{2,1,0:T(8,128)(2,1)}) %reduce-scatter.2.cloned.1.call-update) | async-done | bytes 262160 | tf_op jit(solution)/shard_map/reduce_scatter | solution.py:302
  236.8 1.1 multiply_reduce_fusion
  237.9 9.3 %psum.15 = f32[4,32]{1,0:T(4,128)S(1)} all-reduce(f32[4,32]{1,0:T(4,128)S(1)} %multiply_reduce_fusion), channel_id=1, replica_groups=mesh['grp'=2,'ctx'=4,'head'=4] {'head'}, use_global_device_ids=true, to_apply=%region_5.6 | all-reduce | flops 128 | bytes 1024 | tf_op jit(solution)/shard_map/psum | solution.py:306
  247.2 1.8 multiply_convert_fusion
  (17 shorter events, 0.3 us)
Async XLA Ops:
  6.5 195.1 %all-reduce.2.cloned.1.call-start = ((), (), s32[]{:S(2)}) async-start(), calls=%async_computation.1 | async-start | bytes 1048576 | tf_op jit(solution)/shard_map/psum | solution.py:282
  149.1 11.8 %copy-start = (bf16[3,4096,1024]{2,1,0:T(8,128)(2,1)S(1)}, bf16[3,4096,1024]{2,1,0:T(8,128)(2,1)}, u32[]{:S(2)}) copy-start(bf16[3,4096,1024]{2,1,0:T(8,128)(2,1)} %get-tuple-element.12) | copy-start | bytes 75497472
  160.9 9.2 %copy-start.1 = (bf16[4,32,4096]{2,1,0:T(8,128)(2,1)S(1)}, bf16[4,32,4096]{2,1,0:T(8,128)(2,1)}, u32[]{:S(2)}) copy-start(bf16[4,32,4096]{2,1,0:T(8,128)(2,1)} %get-tuple-element.13) | copy-start | bytes 3145732
  169.8 67.0 %reduce-scatter.2.cloned.1.call-start = ((), (), s32[]{:S(2)}) async-start(), calls=%async_computation.2 | async-start | bytes 1310720 | tf_op jit(solution)/shard_map/reduce_scatter | solution.py:302
  170.4 12.1 %copy-start.3 = (s32[128]{0:T(128)S(1)}, s32[128]{0:T(128)}, u32[]{:S(2)}) copy-start(s32[128]{0:T(128)} %param.11) | copy-start | bytes 1540
  183.3 53.5 %copy-start.2 = (bf16[4,32,1024]{2,1,0:T(8,128)(2,1)S(1)}, bf16[4,32,1024]{2,1,0:T(8,128)(2,1)}, u32[]{:S(2)}) copy-start(bf16[4,32,1024]{2,1,0:T(8,128)(2,1)} %get-tuple-element.10) | copy-start | bytes 786436
Sparse Core Ops, SparseCore 0:
  169.9 31.7 all-reduce.1
  209.3 27.3 reduce-scatter.1

commit v2 on v1

--- a/solution.py
+++ b/solution.py
@@ -36,8 +36,9 @@
     pl.semaphore_wait(barrier, total)
 
 
-def gather_kernel(sizes, p_ref, w_ref, o_ref, looked_ref, pf_ref, wf_ref, of_ref, ef_ref, em_ref,
-                  e_in, own_sem, e_send, e_recv, z_send, z_recv, x_send, x_recv,
+def gather_kernel(sizes, p_ref, w_ref, o_ref, looked_ref, of_ref, em_ref, qkv_ref, state_ref,
+                  xa, wf_ref, ef_ref, kv, s_mine, s_chip, s_half, s_mate, s_far, s_back,
+                  s_send, s_recv, e_in, own_sem, e_send, e_recv, z_send, z_recv, x_send, x_recv,
                   y_send, y_recv, pown_send, pown_recv, px_send, px_recv, py_send, py_recv):
     grp_n, ctx_n, head_n = sizes
     chips = ctx_n // 2
@@ -46,8 +47,11 @@
     partner = {"ctx": chip * 2 + 1 - core}
     kinds, rows, cols = w_ref.shape
     o_rows, o_cols = o_ref.shape
-    width = p_ref.shape[2]
-    resp = em_ref.shape[1]
+    p_rows, width = p_ref.shape
+    steps, resp = em_ref.shape[:2]
+    r_rows = steps * resp
+    heads = cols // DH
+    tile = min(256, cols)
     w_sub = rows // (grp_n * SUB)
     o_sub = o_rows // (grp_n * SUB)
     chunks = [(kind, sub) for kind in (1, 2, 0, 3) for sub in range(SUB)]
@@ -67,7 +71,7 @@
         return w_ref.at[kind, pl.ds(pl.multiple_of((part * SUB + sub) * w_sub, w_sub), w_sub), :]
 
     def prompt_at(owner):
-        return pf_ref.at[:, :, pl.ds(pl.multiple_of(owner * width, width), width)]
+        return xa.at[pl.ds(0, p_rows), pl.ds(pl.multiple_of(owner * width, width), width)]
 
     def embed_at(owner):
         return ef_ref.at[:, :, pl.ds(pl.multiple_of(owner * width, width), width)]
@@ -111,23 +115,35 @@
 
     for way in range(2):
         start_if(z_next[way], z_copy(p_ref, prompt_at(head), 0, way, 1))
-    for index in range(len(chunks)):
+    def x_first(index):
         for way in range(2):
             if chips > 1:
                 start_if(x_next[way], x_copy(chunk_src(index, grp), index, way, 1, ctx))
 
+    for index in range(len(chunks) - 1):
+        x_first(index)
+
     mate = chip * 2 + 1 - core
-    for number, (src, dst) in enumerate(((w_ref, w_at), (o_ref, o_at))):
+    w_ready, x_ready, ef_ready = [], [], []
+    for number, (src, dst, ready) in enumerate(((w_ref, w_at, w_ready), (o_ref, o_at, ends))):
         local = pltpu.make_async_copy(src, dst(ctx), own_sem.at[number])
         local.start()
-        at_end(None, local.wait)
+        ready.append((None, local.wait))
         copy = remote(src, dst(ctx), pown_send.at[number], pown_recv.at[number], partner)
         copy.start()
         at_end(None, copy.wait_send)
-        at_end(None, remote(src, dst(mate), pown_send.at[number], pown_recv.at[number], partner).wait_recv)
+        ready.append((None, remote(src, dst(mate), pown_send.at[number], pown_recv.at[number], partner).wait_recv))
     local = pltpu.make_async_copy(p_ref, prompt_at(head), own_sem.at[2])
     local.start()
-    at_end(None, local.wait)
+    x_ready.append((None, local.wait))
+
+    def settle(waits):
+        for ok, fn in waits:
+            if ok is None:
+                fn()
+            else:
+                pl.when(ok)(fn)
+        waits.clear()
 
     total = looked_ref[:, pl.ds(pl.multiple_of(ctx * resp, resp), resp), :].astype(jnp.float32)
     for step in range(1, ctx_n):
@@ -136,7 +152,7 @@
     em_ref[...] = total.astype(em_ref.dtype)
     local = pltpu.make_async_copy(em_ref, embed_at(head), own_sem.at[3])
     local.start()
-    at_end(None, local.wait)
+    ef_ready.append((None, local.wait))
     for way in range(2):
         start_if(z_next[way], z_copy(em_ref, embed_at(head), 1, way, 1))
 
@@ -164,8 +180,10 @@
         copy = remote(dst, dst, send, recv, partner)
         start_if(ok, copy)
 
-    def mate_wait(ok, dst, send, recv):
-        at_end(ok, remote(dst, dst, send, recv, partner).wait_recv)
+    mate_ready = {kind: [] for kind in range(4)}
+
+    def mate_wait(index, ok, dst, send, recv):
+        mate_ready[chunks[index][0]].append((ok, remote(dst, dst, send, recv, partner).wait_recv))
 
     def x_event(index, way, dist):
         from_chip = chip - dist if way == 0 else chip + dist
@@ -184,7 +202,7 @@
                                   {"grp": lax.rem(grp + step, grp_n)}))
         sems = px_send.at[way, dist - 1, index], px_recv.at[way, dist - 1, index]
         pass_on(have, place, *sems)
-        mate_wait(have, chunk_dst(index, from_chip * 2 + 1 - core, grp), *sems)
+        mate_wait(index, have, chunk_dst(index, from_chip * 2 + 1 - core, grp), *sems)
 
     def y_event(index, way, dist, step):
         from_chip = chip - dist if way == 0 else chip + dist
@@ -199,22 +217,117 @@
 
         sems = py_send.at[key], py_recv.at[key]
         pass_on(have, place, *sems)
-        mate_wait(have, chunk_dst(index, from_chip * 2 + 1 - core, part), *sems)
-
+        mate_wait(index, have, chunk_dst(index, from_chip * 2 + 1 - core, part), *sems)
+
+    def norm_rows():
+        settle(ef_ready)
+        values = ef_ref[...].astype(jnp.float32).reshape(r_rows, ef_ref.shape[2])
+        xa[pl.ds(p_rows, r_rows), :] = rms_rows(values).astype(xa.dtype)
+
+    def project(kind, first, last):
+        settle(x_ready)
+        if kind == 1 and first == 0:
+            settle(w_ready)
+        settle(mate_ready[kind])
+
+        @pl.loop(first, last)
+        def _(number):
+            lanes = pl.ds(pl.multiple_of(number * tile, tile), tile)
+            if kind == 0:
+                rows_in = xa[pl.ds(p_rows, r_rows), :]
+            else:
+                rows_in = xa[...]
+            out = jnp.dot(rows_in, wf_ref[kind, :, lanes], preferred_element_type=jnp.float32)
+            out = out.astype(kv.dtype)
+            if kind == 0:
+                qkv_ref[0, :, lanes] = out
+            else:
+                kv[kind - 1, :, lanes] = out[:p_rows]
+                qkv_ref[kind, :, lanes] = out[p_rows:]
+
+    def to_mate(src, dst, number):
+        return remote(src, dst, s_send.at[number], s_recv.at[number], partner)
+
+    def make_state():
+        span = p_rows // 2
+
+        @pl.loop(0, 2 * heads)
+        def _(number):
+            rows_at = pl.ds(pl.multiple_of(number // heads * span, span), span)
+            lanes = pl.ds(pl.multiple_of(lax.rem(number, heads) * DH, DH), DH)
+            s_chip[number] = lax.dot_general(
+                kv[0, rows_at, lanes], kv[1, rows_at, lanes], (((0,), (0,)), ((), ())),
+                preferred_element_type=jnp.float32,
+            )
+        s_mine[...] = s_chip[...].astype(s_mine.dtype)
+        copy = to_mate(s_mine, s_mate, 0)
+        copy.start()
+        at_end(None, copy.wait_send)
+
+    mine = pl.ds(core * heads, heads)
+    theirs = pl.ds((1 - core) * heads, heads)
+
+    def far_copy(step):
+        other = lax.rem(chip + step, chips)
+        return remote(s_half, s_far.at[step - 1], s_send.at[1 + step], s_recv.at[1 + step],
+                      {"ctx": other * 2 + core})
+
+    def chip_state():
+        to_mate(s_mine, s_mate, 0).wait_recv()
+        s_chip[...] = s_chip[...] + s_mate[...].astype(jnp.float32)
+        s_half[...] = s_chip[mine].astype(s_half.dtype)
+        for step in range(1, chips):
+            copy = far_copy(step)
+            copy.start()
+            at_end(None, copy.wait_send)
+        x_first(len(chunks) - 1)
+
+    def whole_state():
+        total = s_chip[mine]
+        for step in range(1, chips):
+            far_copy(step).wait_recv()
+            total = total + s_far[step - 1].astype(jnp.float32)
+        state_ref[mine] = total
+        s_back[0] = total.astype(s_back.dtype)
+        copy = to_mate(s_back.at[0], s_back.at[1], 1)
+        copy.start()
+        at_end(None, copy.wait_send)
+
+    def mate_state():
+        to_mate(s_back.at[0], s_back.at[1], 1).wait_recv()
+        state_ref[theirs] = s_back[1].astype(jnp.float32)
+
+    ready = 22.0 * (head_n - 1) + 5.5
+    for dist in range(1, chips):
+        ready = max(ready, 11.0 * 2 * SUB + 12.5 + 88.0 * (dist - 1))
+    after = ready + 20.0
     for dist in range(1, chips):
         for index in range(len(chunks)):
             when = 11.0 * (index + 1) + 88.0 * (dist - 1)
+            if index == len(chunks) - 1:
+                when = max(when, after + 12.0 * dist)
             for way in range(2):
                 events.append((when, functools.partial(x_event, index, way, dist)))
                 for step in range(1, grp_n):
                     events.append((when + 12.0, functools.partial(y_event, index, way, dist, step)))
+    tiles = cols // tile
+    cut = (tiles + 1) // 2
+    events.append((ready, norm_rows))
+    for number, kind in enumerate((1, 2)):
+        events.append((ready + 10.0 * number, functools.partial(project, kind, 0, cut)))
+        if cut < tiles:
+            events.append((ready + 10.0 * number + 5.0, functools.partial(project, kind, cut, tiles)))
+    events.append((after, make_state))
+    events.append((after + 2.0, chip_state))
+    last = max(when for when, _ in events)
+    events.append((max(after + 3.0, 11.0 * 3 * SUB + 12.5 + 88.0 * max(chips - 2, 0)),
+                   functools.partial(project, 0, 0, tiles)))
+    events.append((after + 9.0, whole_state))
+    events.append((last + 50.0, mate_state))
     for _, fn in sorted(events, key=lambda event: event[0]):
         fn()
-    for ok, fn in ends:
-        if ok is None:
-            fn()
-        else:
-            pl.when(ok)(fn)
+    settle(mate_ready[3])
+    settle(ends)
 
 
 def gather_all(sizes, prompt_hidden, qkv_weight, out_weight, looked):
@@ -223,6 +336,9 @@
     kinds, rows, cols = qkv_weight.shape
     steps, resp_all, width = looked.shape
     resp = resp_all // ctx_n
+    p_rows = prompt_hidden.shape[0]
+    heads = cols // DH
+    features = width * head_n
     n_chunks = (kinds + 1) * SUB
     dtype = prompt_hidden.dtype
     vmem = pl.BlockSpec(memory_space=pltpu.VMEM)
@@ -231,18 +347,29 @@
     x_sem = pltpu.SemaphoreType.DMA((2, far, n_chunks))
     y_sem = pltpu.SemaphoreType.DMA((2, far, max(grp_n - 1, 1), n_chunks))
     z_sem = pltpu.SemaphoreType.DMA((2, 2, max(head_n - 1, 1)))
+    s_sem = pltpu.SemaphoreType.DMA((1 + chips,))
     return pl.pallas_call(
         functools.partial(gather_kernel, sizes),
         out_shape=(
-            jax.ShapeDtypeStruct(prompt_hidden.shape[:2] + (width * head_n,), dtype),
-            jax.ShapeDtypeStruct((kinds, rows * ctx_n, cols), dtype),
             jax.ShapeDtypeStruct((out_weight.shape[0], out_weight.shape[1] * ctx_n), dtype),
-            jax.ShapeDtypeStruct((steps, resp, width * head_n), dtype),
             jax.ShapeDtypeStruct((steps, resp, width), dtype),
+            jax.ShapeDtypeStruct((kinds, steps * resp, cols), dtype),
+            jax.ShapeDtypeStruct((2 * heads, DH, DH), jnp.float32),
         ),
-        in_specs=[vmem] * 4,
-        out_specs=(hbm, hbm, hbm, hbm, vmem),
+        in_specs=[hbm, hbm, vmem, vmem],
+        out_specs=(hbm, vmem, vmem, vmem),
         scratch_shapes=[
+            pltpu.VMEM((p_rows + steps * resp, features), dtype),
+            pltpu.VMEM((kinds, rows * ctx_n, cols), dtype),
+            pltpu.VMEM((steps, resp, features), dtype),
+            pltpu.VMEM((2, p_rows, cols), dtype),
+            pltpu.VMEM((2 * heads, DH, DH), dtype),
+            pltpu.VMEM((2 * heads, DH, DH), jnp.float32),
+            pltpu.VMEM((heads, DH, DH), dtype),
+            pltpu.VMEM((2 * heads, DH, DH), dtype),
+            pltpu.VMEM((far, heads, DH, DH), dtype),
+            pltpu.VMEM((2, heads, DH, DH), dtype),
+            s_sem, s_sem,
             pltpu.VMEM((ctx_n - 1, steps, resp, width), dtype),
             pltpu.SemaphoreType.DMA((4,)),
             pltpu.SemaphoreType.DMA((ctx_n - 1,)),
@@ -251,8 +378,69 @@
             pltpu.SemaphoreType.DMA((2,)), pltpu.SemaphoreType.DMA((2,)),
             x_sem, x_sem, y_sem, y_sem,
         ],
-        compiler_params=pltpu.CompilerParams(collective_id=0, has_side_effects=True),
+        compiler_params=pltpu.CompilerParams(
+            collective_id=0, has_side_effects=True, vmem_limit_bytes=62 * 1024 * 1024
+        ),
     )(prompt_hidden, qkv_weight, out_weight, looked)
+
+
+def finish_kernel(head_n, t_ref, em_ref, out_ref, parts, squares, far_squares,
+                  t_send, t_recv, q_send, q_recv):
+    head = lax.axis_index("head")
+    width = em_ref.shape[2]
+    greet((("head", head_n),))
+
+    def block(owner):
+        return pl.ds(pl.multiple_of(owner * width, width), width)
+
+    def term_copy(step):
+        to = lax.rem(head + step, head_n)
+        return remote(t_ref.at[:, :, block(to)], parts.at[step - 1],
+                      t_send.at[step - 1], t_recv.at[step - 1], {"head": to})
+
+    def square_copy(step):
+        to = lax.rem(head + step, head_n)
+        return remote(squares, far_squares.at[step - 1],
+                      q_send.at[step - 1], q_recv.at[step - 1], {"head": to})
+
+    for step in range(1, head_n):
+        term_copy(step).start()
+    mixed = em_ref[...].astype(jnp.float32) + t_ref[:, :, block(head)].astype(jnp.float32)
+    for step in range(1, head_n):
+        term_copy(step).wait_recv()
+        mixed += parts[step - 1].astype(jnp.float32)
+    total = jnp.broadcast_to(jnp.sum(mixed * mixed, axis=-1, keepdims=True), squares.shape)
+    squares[...] = total
+    for step in range(1, head_n):
+        square_copy(step).start()
+    for step in range(1, head_n):
+        square_copy(step).wait_recv()
+        total += far_squares[step - 1]
+    scale = lax.rsqrt(total[:, :, :1] / (width * head_n) + 1e-06)
+    out_ref[...] = (mixed * scale).astype(out_ref.dtype)
+    for step in range(1, head_n):
+        term_copy(step).wait_send()
+        square_copy(step).wait_send()
+
+
+def finish(head_n, terms, embedded_mine):
+    steps, resp, width = embedded_mine.shape
+    vmem = pl.BlockSpec(memory_space=pltpu.VMEM)
+    others = max(head_n - 1, 1)
+    sem = pltpu.SemaphoreType.DMA((others,))
+    return pl.pallas_call(
+        functools.partial(finish_kernel, head_n),
+        out_shape=jax.ShapeDtypeStruct(embedded_mine.shape, jnp.bfloat16),
+        in_specs=[vmem, vmem],
+        out_specs=vmem,
+        scratch_shapes=[
+            pltpu.VMEM((others,) + embedded_mine.shape, jnp.bfloat16),
+            pltpu.VMEM((steps, resp, 128), jnp.float32),
+            pltpu.VMEM((others, steps, resp, 128), jnp.float32),
+            sem, sem, sem, sem,
+        ],
+        compiler_params=pltpu.CompilerParams(collective_id=1, has_side_effects=True),
+    )(terms, embedded_mine)
 
 
 def on_device(sizes, prompt_hidden, qkv_weight, out_weight, embed_table, response_ids, assignment):
@@ -268,26 +456,14 @@
     inside = (offset_ids >= 0) & (offset_ids < vocab_rows)
     looked = jnp.take(embed_table, jnp.clip(offset_ids, 0, vocab_rows - 1), axis=0)
     looked = jnp.where(inside[:, :, None], looked, jnp.zeros((), looked.dtype))
-    piece, full_rows, full_out, embedded, embedded_mine = gather_all(
-        sizes, prompt_hidden, qkv_weight, out_weight, looked
+    full_out, embedded_mine, projected_qkv, state = gather_all(
+        sizes, prompt_hidden.reshape(2 * prompt_rows, local_cols), qkv_weight, out_weight, looked
     )
-    flat_piece = piece.reshape(2 * prompt_rows, piece.shape[2])
-    keys = jnp.dot(flat_piece, full_rows[1], preferred_element_type=jnp.float32)
-    keys = keys.astype(jnp.bfloat16).reshape(2, prompt_rows, local_heads, head_size)
-    values = jnp.dot(flat_piece, full_rows[2], preferred_element_type=jnp.float32)
-    values = values.astype(jnp.bfloat16).reshape(2, prompt_rows, local_heads, head_size)
-    partial_state = jnp.einsum(
-        "pthd,pthe->phde", keys, values, preferred_element_type=jnp.float32
-    )
-    state = lax.psum(partial_state.astype(jnp.bfloat16), "ctx").astype(jnp.float32)
-    normed = rms_rows(embedded.astype(jnp.float32)).astype(jnp.bfloat16)
-    projected_qkv = jnp.einsum(
-        "trd,kde->trke", normed, full_rows, preferred_element_type=jnp.float32
-    ).astype(jnp.bfloat16)
-    projected_qkv = projected_qkv.reshape(steps, resp_local, 3, local_heads, head_size)
-    query = projected_qkv[:, :, 0]
-    key = projected_qkv[:, :, 1]
-    value = projected_qkv[:, :, 2]
+    state = state.reshape(2, local_heads, head_size, head_size)
+    projected_qkv = projected_qkv.reshape(3, steps, resp_local, local_heads, head_size)
+    query = projected_qkv[0]
+    key = projected_qkv[1]
+    value = projected_qkv[2]
     my_prompt = lax.dynamic_slice_in_dim(assignment, ctx_index * resp_local, resp_local, 0)
     query_f = query.astype(jnp.float32)
     both = jnp.einsum("trhd,phde->ptrhe", query_f, state, precision=lax.Precision.HIGHEST)
@@ -298,14 +474,7 @@
     local = jnp.einsum("rhts,srhd->trhd", scores, value, preferred_element_type=jnp.float32)
     head_out = rms_rows(chosen + local).astype(jnp.bfloat16).reshape(steps, resp_local, local_cols)
     terms = jnp.einsum("trd,de->tre", head_out, full_out, preferred_element_type=jnp.float32)
-    width = terms.shape[2]
-    mine = lax.psum_scatter(
-        terms.astype(jnp.bfloat16), "head", scatter_dimension=2, tiled=True
-    ).astype(jnp.float32)
-    mixed = embedded_mine.astype(jnp.float32) + mine
-    squares = lax.psum(jnp.sum(mixed * mixed, axis=-1), "head")
-    result = mixed * lax.rsqrt(squares[:, :, None] / width + 1e-06)
-    return result.astype(jnp.bfloat16)
+    return finish(sizes[2], terms.astype(jnp.bfloat16), embedded_mine)
 
 
 def solution(mesh):

time: 256 us -> 214 us (0.84)
  Pallas kernels: 129 us -> 189 us
  waiting for transfers between devices: 46 us -> 0 us
  matrix products: 37.1 us -> 8.35 us
  between operations: 13.5 us -> 0.1 us
  blocking collectives: 9.28 us -> 0 us
  other arithmetic: 6.31 us -> 3.2 us
    pallas_call x0 -> x1, Pallas kernels: none -> 36.2 us  [finish(): pl.pallas_call(functools.partial(finish_kernel, head_n), out_shape=jax.Sh...]
    dot_general x4 -> x0, matrix products: 29.4 us -> none  [the longest x1 11.8 us: on_device(): jnp.einsum('trd,kde->trke', normed, full_rows, preferred_element_type=jnp...]
    reduce_scatter x1 -> x0, waiting for transfers between devices: 27.6 us -> none  [on_device(): lax.psum_scatter(terms.astype(jnp.bfloat16), 'head', scatter_dimension=2,...]
    pallas_call x1, Pallas kernels: 129 us -> 153 us  [gather_all(): pl.pallas_call(functools.partial(gather_kernel, sizes), out_shape=(jax.Sh...]
    psum x1 -> x0, waiting for transfers between devices: 18.4 us -> none  [on_device(): lax.psum(partial_state.astype(jnp.bfloat16), 'ctx').astype(jnp.float32)]
    psum x1 -> x0, blocking collectives: 9.28 us -> none  [on_device(): squares = lax.psum(jnp.sum(mixed * mixed, axis=-1), 'head')]
  transfers between devices with their start and end apart: 2 -> 0, of which waited for: 2 -> 0; matrix products, arithmetic and copies ran while one was open for 5% -> 0% of each run, Pallas kernels for 0% -> 0%
where the time goes in v2:
time: 214 us
  Pallas kernels  189 us (88%)
  local copies, waits for them, and re-layouts  13.7 us (6%)
  matrix products  8.35 us (4%)
  other arithmetic  3.2 us (1%)
    pallas_call x1, Pallas kernels, gather_all(): pl.pallas_call(functools.partial(gather_kernel, sizes), out_shape=(jax.Sh...  153 us
    pallas_call x1, Pallas kernels, finish(): pl.pallas_call(functools.partial(finish_kernel, head_n), out_shape=jax.Sh...  36.2 us
    gather x1, local copies, waits for them, and re-layouts, on_device(): jnp.take(embed_table, jnp.clip(offset_ids, 0, vocab_rows - 1), axis=0)  10.7 us
    dot_general x1, matrix products, on_device(): jnp.einsum('trd,de->tre', head_out, full_out, preferred_element_type=jnp....  5.75 us

profile of v2, /device:TPU:0, one launch (start us, length us, event | category | flops | bytes accessed | tf_op | source)
XLA Modules:
  0.0 214.1 jit_solution(4819968638775423667)
XLA Ops:
  0.0 0.7 compare_and_fusion.1
  0.7 0.7 fusion.21
  1.4 10.7 %gather_fusion = bf16[512,1024]{1,0:T(8,128)(2,1)S(1)} fusion(bf16[8192,1024]{1,0:T(8,128)(2,1)} %param.9, s32[1024]{0:T(1024)S(1)} %pad_clamp_fusion), kind=kCustom, calls=%fused_computation | custom fusion | bytes 2099200 | tf_op jit(solution)/shard_map/jit(_take)/gather | solution.py:457
  12.1 1.3 select_select_fusion.looked_ref
  13.3 0.0 copy-start
  13.3 152.6 %shard_map.64 = (bf16[1024,4096]{1,0:T(8,128)(2,1)}, bf16[4,32,1024]{2,1,0:T(8,128)(2,1)}, bf16[3,128,1024]{2,1,0:T(8,128)(2,1)}, f32[16,128,128]{2,1,0:T(8,128)}) custom-call(bf16[512,1024]{1,0:T(8,128)(2,1)} %bitcast.58, bf16[3,1024,1024]{2,1,0:T(8,128)(2,1)} %w_ref.1, bf16[1024,1024]{1,0:T(8,128)(2,1)} %o_ref.1, ...), custom_call_target="tpu_custom_call" | custom-call | tf_op jit(solution)/shard_map/pallas_call | solution.py:351
  166.0 1.2 slice_bitcast_fusion.3
  167.3 0.7 fusion.6
  168.1 1.9 convolution_bitcast_fusion
  170.0 0.0 copy-done
  170.0 0.1 dynamic-slice_compare_fusion
  170.1 0.4 multiply_reduce_fusion
  170.5 5.8 %fusion.2.t_ref = bf16[4,32,4096]{2,1,0:T(8,128)(2,1)} fusion(bf16[1024,4096]{1,0:T(8,128)(2,1)} %get-tuple-element.11, f32[4,32,8,128]{3,1,0,2:T(8,128)S(1)} %get-tuple-element.14, f32[4,32,8]{1,0,2:T(4,128)S(1)} %add_rsqrt_fusion), kind=kOutput, calls=%fused_computation.3 | convolution fusion | flops 1074528256 | bytes 9965568 | tf_op jit(solution)/shard_map/trd,de->tre/dot_general | solution.py:476
  176.3 36.2 %shard_map.65 = bf16[4,32,1024]{2,1,0:T(8,128)(2,1)} custom-call(bf16[4,32,4096]{2,1,0:T(8,128)(2,1)} %fusion.2.t_ref, bf16[4,32,1024]{2,1,0:T(8,128)(2,1)} %get-tuple-element.12.em_ref), custom_call_target="tpu_custom_call" | custom-call | tf_op jit(solution)/shard_map/pallas_call | solution.py:431
  212.4 1.7 copy.50
  (7 shorter events, 0.2 us)
Async XLA Ops:
  13.3 156.6 %copy-start = (s32[128]{0:T(128)S(1)}, s32[128]{0:T(128)}, u32[]{:S(2)}) copy-start(s32[128]{0:T(128)} %param.11) | copy-start | bytes 1540

commit v3 on v2

--- a/solution.py
+++ b/solution.py
@@ -36,8 +36,8 @@
     pl.semaphore_wait(barrier, total)
 
 
-def gather_kernel(sizes, p_ref, w_ref, o_ref, looked_ref, of_ref, em_ref, qkv_ref, state_ref,
-                  xa, wf_ref, ef_ref, kv, s_mine, s_chip, s_half, s_mate, s_far, s_back,
+def gather_kernel(sizes, p_ref, w_ref, o_ref, ids_ref, table_ref, of_ref, em_ref, qkv_ref, state_ref,
+                  xa, wf_ref, ef_ref, acc, found, looked_ref, t_tile, t_sem, s_mine, s_chip, s_half, s_mate, s_far, s_back,
                   s_send, s_recv, e_in, own_sem, e_send, e_recv, z_send, z_recv, x_send, x_recv,
                   y_send, y_recv, pown_send, pown_recv, px_send, px_recv, py_send, py_recv):
     grp_n, ctx_n, head_n = sizes
@@ -52,6 +52,7 @@
     r_rows = steps * resp
     heads = cols // DH
     tile = min(256, cols)
+    tiles = cols // tile
     w_sub = rows // (grp_n * SUB)
     o_sub = o_rows // (grp_n * SUB)
     chunks = [(kind, sub) for kind in (1, 2, 0, 3) for sub in range(SUB)]
@@ -89,15 +90,6 @@
     def at_end(ok, fn):
         ends.append((ok, fn))
 
-    for step in range(1, ctx_n):
-        to = lax.rem(ctx + step, ctx_n)
-        copy = remote(
-            looked_ref.at[:, pl.ds(pl.multiple_of(to * resp, resp), resp), :], e_in.at[step - 1],
-            e_send.at[step - 1], e_recv.at[step - 1], {"ctx": to},
-        )
-        copy.start()
-        at_end(None, copy.wait_send)
-
     def x_copy(src, index, way, dist, shard):
         return remote(src, chunk_dst(index, shard, grp), x_send.at[way, dist - 1, index],
                       x_recv.at[way, dist - 1, index], {"ctx": ctx + (2 if way == 0 else -2)})
@@ -120,7 +112,7 @@
             if chips > 1:
                 start_if(x_next[way], x_copy(chunk_src(index, grp), index, way, 1, ctx))
 
-    for index in range(len(chunks) - 1):
+    for index in range(2):
         x_first(index)
 
     mate = chip * 2 + 1 - core
@@ -145,18 +137,58 @@
                 pl.when(ok)(fn)
         waits.clear()
 
-    total = looked_ref[:, pl.ds(pl.multiple_of(ctx * resp, resp), resp), :].astype(jnp.float32)
-    for step in range(1, ctx_n):
-        remote(e_in.at[step - 1], e_in.at[step - 1], e_send.at[step - 1], e_recv.at[step - 1], partner).wait_recv()
-        total += e_in[step - 1].astype(jnp.float32)
-    em_ref[...] = total.astype(em_ref.dtype)
-    local = pltpu.make_async_copy(em_ref, embed_at(head), own_sem.at[3])
-    local.start()
-    ef_ready.append((None, local.wait))
-    for way in range(2):
-        start_if(z_next[way], z_copy(em_ref, embed_at(head), 1, way, 1))
-
     events = []
+
+    vocab = table_ref.shape[0]
+    t_rows = t_tile.shape[1]
+    n_tiles = vocab // t_rows
+
+    def tile_copy(number, slot):
+        start = pl.multiple_of(number * t_rows, t_rows)
+        return pltpu.make_async_copy(table_ref.at[pl.ds(start, t_rows), :], t_tile.at[slot], t_sem.at[slot])
+
+    def lookup(first, last):
+        tile_copy(first, first % 2).start()
+        if first == 0:
+            found[...] = jnp.zeros_like(found)
+
+        @pl.loop(first, last)
+        def _(number):
+            slot = lax.rem(number, 2)
+
+            @pl.when(number + 1 < last)
+            def _():
+                tile_copy(number + 1, lax.rem(number + 1, 2)).start()
+
+            tile_copy(number, slot).wait()
+            names = lax.broadcasted_iota(jnp.int32, (ids_ref.shape[0], t_rows), 1)
+            hits = ids_ref[...] == names + (ctx * vocab + number * t_rows)
+            pick = jnp.where(hits, 1.0, 0.0).astype(looked_ref.dtype)
+            found[...] += jnp.dot(pick, t_tile[slot], preferred_element_type=jnp.float32)
+
+    def embed_send():
+        looked_ref[...] = found[...].astype(looked_ref.dtype).reshape(looked_ref.shape)
+        for step in range(1, ctx_n):
+            to = lax.rem(ctx + step, ctx_n)
+            copy = remote(
+                looked_ref.at[:, pl.ds(pl.multiple_of(to * resp, resp), resp), :], e_in.at[step - 1],
+                e_send.at[step - 1], e_recv.at[step - 1], {"ctx": to},
+            )
+            copy.start()
+            at_end(None, copy.wait_send)
+        x_first(2)
+
+    def embed_sum():
+        total = looked_ref[:, pl.ds(pl.multiple_of(ctx * resp, resp), resp), :].astype(jnp.float32)
+        for step in range(1, ctx_n):
+            remote(e_in.at[step - 1], e_in.at[step - 1], e_send.at[step - 1], e_recv.at[step - 1], partner).wait_recv()
+            total += e_in[step - 1].astype(jnp.float32)
+        em_ref[...] = total.astype(em_ref.dtype)
+        local = pltpu.make_async_copy(em_ref, embed_at(head), own_sem.at[3])
+        local.start()
+        ef_ready.append((None, local.wait))
+        for way in range(2):
+            start_if(z_next[way], z_copy(em_ref, embed_at(head), 1, way, 1))
 
     def z_event(what, way, dist):
         owner = head - dist if way == 0 else head + dist
@@ -174,7 +206,7 @@
     for dist in range(1, head_n):
         for way in range(2):
             events.append((22.0 * dist, functools.partial(z_event, 0, way, dist)))
-            events.append((22.0 * dist + 5.0, functools.partial(z_event, 1, way, dist)))
+            events.append((22.0 * dist + 20.0, functools.partial(z_event, 1, way, dist)))
 
     def pass_on(ok, dst, send, recv):
         copy = remote(dst, dst, send, recv, partner)
@@ -189,6 +221,8 @@
         from_chip = chip - dist if way == 0 else chip + dist
         have = from_chip >= 0 if way == 0 else from_chip < chips
         place = chunk_dst(index, from_chip * 2 + core, grp)
+        if way == 0 and dist == 1 and 1 <= index < len(chunks) - 2:
+            x_first(index + 2)
 
         @pl.when(have)
         def _():
@@ -224,26 +258,41 @@
         values = ef_ref[...].astype(jnp.float32).reshape(r_rows, ef_ref.shape[2])
         xa[pl.ds(p_rows, r_rows), :] = rms_rows(values).astype(xa.dtype)
 
-    def project(kind, first, last):
+    def lanes_of(number):
+        return pl.ds(pl.multiple_of(number * tile, tile), tile)
+
+    def prompt_dots(dist):
         settle(x_ready)
-        if kind == 1 and first == 0:
-            settle(w_ready)
+        settle(w_ready)
+        settle(mate_ready[1])
+        settle(mate_ready[2])
+        for way in range(2 if dist else 1):
+            owner = head - dist if way == 0 else head + dist
+            have = owner >= 0 if way == 0 else owner < head_n
+            block = pl.ds(pl.multiple_of(owner * width, width), width)
+
+            @pl.when(have)
+            def _():
+                @pl.loop(0, 2 * tiles)
+                def _(number):
+                    kind = number // tiles
+                    lanes = lanes_of(lax.rem(number, tiles))
+                    out = jnp.dot(xa[pl.ds(0, p_rows), block], wf_ref[1 + kind, block, lanes],
+                                  preferred_element_type=jnp.float32)
+                    if dist:
+                        acc[kind, :, lanes] += out
+                    else:
+                        acc[kind, :, lanes] = out
+
+    def project(kind):
         settle(mate_ready[kind])
 
-        @pl.loop(first, last)
+        @pl.loop(0, tiles)
         def _(number):
-            lanes = pl.ds(pl.multiple_of(number * tile, tile), tile)
-            if kind == 0:
-                rows_in = xa[pl.ds(p_rows, r_rows), :]
-            else:
-                rows_in = xa[...]
-            out = jnp.dot(rows_in, wf_ref[kind, :, lanes], preferred_element_type=jnp.float32)
-            out = out.astype(kv.dtype)
-            if kind == 0:
-                qkv_ref[0, :, lanes] = out
-            else:
-                kv[kind - 1, :, lanes] = out[:p_rows]
-                qkv_ref[kind, :, lanes] = out[p_rows:]
+            lanes = lanes_of(number)
+            out = jnp.dot(xa[pl.ds(p_rows, r_rows), :], wf_ref[kind, :, lanes],
+                          preferred_element_type=jnp.float32)
+            qkv_ref[kind, :, lanes] = out.astype(qkv_ref.dtype)
 
     def to_mate(src, dst, number):
         return remote(src, dst, s_send.at[number], s_recv.at[number], partner)
@@ -256,7 +305,7 @@
             rows_at = pl.ds(pl.multiple_of(number // heads * span, span), span)
             lanes = pl.ds(pl.multiple_of(lax.rem(number, heads) * DH, DH), DH)
             s_chip[number] = lax.dot_general(
-                kv[0, rows_at, lanes], kv[1, rows_at, lanes], (((0,), (0,)), ((), ())),
+                acc[0, rows_at, lanes].astype(s_mine.dtype), acc[1, rows_at, lanes].astype(s_mine.dtype), (((0,), (0,)), ((), ())),
                 preferred_element_type=jnp.float32,
             )
         s_mine[...] = s_chip[...].astype(s_mine.dtype)
@@ -280,7 +329,6 @@
             copy = far_copy(step)
             copy.start()
             at_end(None, copy.wait_send)
-        x_first(len(chunks) - 1)
 
     def whole_state():
         total = s_chip[mine]
@@ -297,32 +345,36 @@
         to_mate(s_back.at[0], s_back.at[1], 1).wait_recv()
         state_ref[theirs] = s_back[1].astype(jnp.float32)
 
-    ready = 22.0 * (head_n - 1) + 5.5
-    for dist in range(1, chips):
-        ready = max(ready, 11.0 * 2 * SUB + 12.5 + 88.0 * (dist - 1))
-    after = ready + 20.0
+    def reach(chunk):
+        return 11.0 * (chunk + 1) + 88.0 * max(chips - 2, 0) + 12.5
+
+    middle = n_tiles // 2
+    events.append((0.0, functools.partial(lookup, 0, middle)))
+    events.append((11.5, functools.partial(lookup, middle, n_tiles)))
+    events.append((11.6, embed_send))
+    events.append((30.0, embed_sum))
     for dist in range(1, chips):
         for index in range(len(chunks)):
             when = 11.0 * (index + 1) + 88.0 * (dist - 1)
-            if index == len(chunks) - 1:
-                when = max(when, after + 12.0 * dist)
             for way in range(2):
                 events.append((when, functools.partial(x_event, index, way, dist)))
                 for step in range(1, grp_n):
                     events.append((when + 12.0, functools.partial(y_event, index, way, dist, step)))
-    tiles = cols // tile
-    cut = (tiles + 1) // 2
-    events.append((ready, norm_rows))
-    for number, kind in enumerate((1, 2)):
-        events.append((ready + 10.0 * number, functools.partial(project, kind, 0, cut)))
-        if cut < tiles:
-            events.append((ready + 10.0 * number + 5.0, functools.partial(project, kind, cut, tiles)))
-    events.append((after, make_state))
-    events.append((after + 2.0, chip_state))
+    ready = reach(2 * SUB - 1)
+    after = ready
+    for dist in range(head_n):
+        after = max(ready + 0.1 * dist, 22.0 * dist + 0.5)
+        events.append((after, functools.partial(prompt_dots, dist)))
+    embedded_at = 22.0 * (head_n - 1) + 20.5
+    events.append((after + 0.1, make_state))
+    events.append((after + 0.2, chip_state))
+    after = max(after + 0.3, embedded_at)
+    events.append((after, norm_rows))
+    events.append((after + 0.2, functools.partial(project, 1)))
+    events.append((after + 3.0, functools.partial(project, 2)))
+    events.append((max(after + 6.0, reach(3 * SUB - 1)), functools.partial(project, 0)))
+    events.append((max(after + 12.0, reach(4 * SUB - 1) - 6.0), whole_state))
     last = max(when for when, _ in events)
-    events.append((max(after + 3.0, 11.0 * 3 * SUB + 12.5 + 88.0 * max(chips - 2, 0)),
-                   functools.partial(project, 0, 0, tiles)))
-    events.append((after + 9.0, whole_state))
     events.append((last + 50.0, mate_state))
     for _, fn in sorted(events, key=lambda event: event[0]):
         fn()
@@ -330,11 +382,12 @@
     settle(ends)
 
 
-def gather_all(sizes, prompt_hidden, qkv_weight, out_weight, looked):
+def gather_all(sizes, prompt_hidden, qkv_weight, out_weight, response_ids, embed_table):
     grp_n, ctx_n, head_n = sizes
     chips = ctx_n // 2
     kinds, rows, cols = qkv_weight.shape
-    steps, resp_all, width = looked.shape
+    steps, resp_all = response_ids.shape
+    width = prompt_hidden.shape[1]
     resp = resp_all // ctx_n
     p_rows = prompt_hidden.shape[0]
     heads = cols // DH
@@ -356,13 +409,17 @@
             jax.ShapeDtypeStruct((kinds, steps * resp, cols), dtype),
             jax.ShapeDtypeStruct((2 * heads, DH, DH), jnp.float32),
         ),
-        in_specs=[hbm, hbm, vmem, vmem],
+        in_specs=[hbm, hbm, vmem, vmem, hbm],
         out_specs=(hbm, vmem, vmem, vmem),
         scratch_shapes=[
             pltpu.VMEM((p_rows + steps * resp, features), dtype),
             pltpu.VMEM((kinds, rows * ctx_n, cols), dtype),
             pltpu.VMEM((steps, resp, features), dtype),
-            pltpu.VMEM((2, p_rows, cols), dtype),
+            pltpu.VMEM((2, p_rows, cols), jnp.float32),
+            pltpu.VMEM((steps * resp_all, width), jnp.float32),
+            pltpu.VMEM((steps, resp_all, width), dtype),
+            pltpu.VMEM((2, min(512, embed_table.shape[0] // 2), width), dtype),
+            pltpu.SemaphoreType.DMA((2,)),
             pltpu.VMEM((2 * heads, DH, DH), dtype),
             pltpu.VMEM((2 * heads, DH, DH), jnp.float32),
             pltpu.VMEM((heads, DH, DH), dtype),
@@ -381,35 +438,55 @@
         compiler_params=pltpu.CompilerParams(
             collective_id=0, has_side_effects=True, vmem_limit_bytes=62 * 1024 * 1024
         ),
-    )(prompt_hidden, qkv_weight, out_weight, looked)
-
-
-def finish_kernel(head_n, t_ref, em_ref, out_ref, parts, squares, far_squares,
+    )(prompt_hidden, qkv_weight, out_weight, response_ids.reshape(-1, 1), embed_table)
+
+
+def finish_kernel(head_n, t_ref, em_ref, out_ref, mixed, sums, parts, squares, far_squares,
                   t_send, t_recv, q_send, q_recv):
     head = lax.axis_index("head")
     width = em_ref.shape[2]
     greet((("head", head_n),))
-
-    def block(owner):
-        return pl.ds(pl.multiple_of(owner * width, width), width)
-
-    def term_copy(step):
-        to = lax.rem(head + step, head_n)
-        return remote(t_ref.at[:, :, block(to)], parts.at[step - 1],
-                      t_send.at[step - 1], t_recv.at[step - 1], {"head": to})
+    go = (head + 1 < head_n, head > 0)
+    have = (head > 0, head + 1 < head_n)
+
+    def term_copy(src, way, to):
+        return remote(src, parts.at[way, to], t_send.at[way, to], t_recv.at[way, to],
+                      {"head": head + (1 if way == 0 else -1)})
 
     def square_copy(step):
         to = lax.rem(head + step, head_n)
         return remote(squares, far_squares.at[step - 1],
                       q_send.at[step - 1], q_recv.at[step - 1], {"head": to})
 
-    for step in range(1, head_n):
-        term_copy(step).start()
-    mixed = em_ref[...].astype(jnp.float32) + t_ref[:, :, block(head)].astype(jnp.float32)
-    for step in range(1, head_n):
-        term_copy(step).wait_recv()
-        mixed += parts[step - 1].astype(jnp.float32)
-    total = jnp.broadcast_to(jnp.sum(mixed * mixed, axis=-1, keepdims=True), squares.shape)
+    order = []
+    for step in range(head_n - 1):
+        order += [(0, head_n - 1 - step), (1, step)]
+    for way, to in order:
+        ahead = to > head if way == 0 else to < head
+        own = t_ref.at[:, :, pl.ds(to * width, width)]
+
+        @pl.when(ahead & have[way])
+        def _():
+            term_copy(sums.at[way, to], way, to).wait_recv()
+            total = own[...].astype(jnp.float32) + parts[way, to].astype(jnp.float32)
+            sums[way, to] = total.astype(sums.dtype)
+            term_copy(sums.at[way, to], way, to).start()
+
+        @pl.when(ahead & jnp.logical_not(have[way]))
+        def _():
+            term_copy(own, way, to).start()
+
+    mixed[...] = em_ref[...].astype(jnp.float32) + t_ref[
+        :, :, pl.ds(pl.multiple_of(head * width, width), width)
+    ].astype(jnp.float32)
+    for way in range(2):
+        @pl.when(have[way])
+        def _():
+            term_copy(sums.at[way, 0], way, head).wait_recv()
+            mixed[...] += parts[way, head].astype(jnp.float32)
+
+    values = mixed[...]
+    total = jnp.broadcast_to(jnp.sum(values * values, axis=-1, keepdims=True), squares.shape)
     squares[...] = total
     for step in range(1, head_n):
         square_copy(step).start()
@@ -417,9 +494,14 @@
         square_copy(step).wait_recv()
         total += far_squares[step - 1]
     scale = lax.rsqrt(total[:, :, :1] / (width * head_n) + 1e-06)
-    out_ref[...] = (mixed * scale).astype(out_ref.dtype)
+    out_ref[...] = (values * scale).astype(out_ref.dtype)
+    for way, to in order:
+        ahead = to > head if way == 0 else to < head
+
+        @pl.when(ahead)
+        def _():
+            term_copy(sums.at[way, to], way, to).wait_send()
     for step in range(1, head_n):
-        term_copy(step).wait_send()
         square_copy(step).wait_send()
 
 
@@ -428,16 +510,19 @@
     vmem = pl.BlockSpec(memory_space=pltpu.VMEM)
     others = max(head_n - 1, 1)
     sem = pltpu.SemaphoreType.DMA((others,))
+    t_sem = pltpu.SemaphoreType.DMA((2, head_n))
     return pl.pallas_call(
         functools.partial(finish_kernel, head_n),
         out_shape=jax.ShapeDtypeStruct(embedded_mine.shape, jnp.bfloat16),
         in_specs=[vmem, vmem],
         out_specs=vmem,
         scratch_shapes=[
-            pltpu.VMEM((others,) + embedded_mine.shape, jnp.bfloat16),
+            pltpu.VMEM(embedded_mine.shape, jnp.float32),
+            pltpu.VMEM((2, head_n) + embedded_mine.shape, jnp.bfloat16),
+            pltpu.VMEM((2, head_n) + embedded_mine.shape, jnp.bfloat16),
             pltpu.VMEM((steps, resp, 128), jnp.float32),
             pltpu.VMEM((others, steps, resp, 128), jnp.float32),
-            sem, sem, sem, sem,
+            t_sem, t_sem, sem, sem,
         ],
         compiler_params=pltpu.CompilerParams(collective_id=1, has_side_effects=True),
     )(terms, embedded_mine)
@@ -451,13 +536,9 @@
     steps = response_ids.shape[0]
     resp_local = response_ids.shape[1] // lax.axis_size("ctx")
     ctx_index = lax.axis_index("ctx")
-    vocab_rows = embed_table.shape[0]
-    offset_ids = response_ids - ctx_index * vocab_rows
-    inside = (offset_ids >= 0) & (offset_ids < vocab_rows)
-    looked = jnp.take(embed_table, jnp.clip(offset_ids, 0, vocab_rows - 1), axis=0)
-    looked = jnp.where(inside[:, :, None], looked, jnp.zeros((), looked.dtype))
     full_out, embedded_mine, projected_qkv, state = gather_all(
-        sizes, prompt_hidden.reshape(2 * prompt_rows, local_cols), qkv_weight, out_weight, looked
+        sizes, prompt_hidden.reshape(2 * prompt_rows, local_cols), qkv_weight, out_weight,
+        response_ids, embed_table,
     )
     state = state.reshape(2, local_heads, head_size, head_size)
     projected_qkv = projected_qkv.reshape(3, steps, resp_local, local_heads, head_size)

time: 214 us -> 185 us (0.86)
  Pallas kernels: 189 us -> 171 us
  local copies, waits for them, and re-layouts: 13.7 us -> 4.53 us
  other arithmetic: 3.2 us -> 0.53 us
    pallas_call x1, Pallas kernels: 153 us -> 131 us  [gather_all(): pl.pallas_call(functools.partial(gather_kernel, sizes), out_shape=(jax.Sh...]
    gather x1 -> x0, local copies, waits for them, and re-layouts: 10.7 us -> none  [on_device(): jnp.take(embed_table, jnp.clip(offset_ids, 0, vocab_rows - 1), axis=0)]
    pallas_call x1, Pallas kernels: 36.2 us -> 40.6 us  [finish(): pl.pallas_call(functools.partial(finish_kernel, head_n), out_shape=jax.Sh...]
where the time goes in v3:
time: 185 us
  Pallas kernels  171 us (92%)
  matrix products  8.34 us (5%)
  local copies, waits for them, and re-layouts  4.53 us (2%)
    pallas_call x1, Pallas kernels, gather_all(): pl.pallas_call(functools.partial(gather_kernel, sizes), out_shape=(jax.Sh...  131 us
    pallas_call x1, Pallas kernels, finish(): pl.pallas_call(functools.partial(finish_kernel, head_n), out_shape=jax.Sh...  40.6 us
    dot_general x1, matrix products, on_device(): jnp.einsum('trd,de->tre', head_out, full_out, preferred_element_type=jnp....  5.75 us

profile of v3, /device:TPU:0, one launch (start us, length us, event | category | flops | bytes accessed | tf_op | source)
XLA Modules:
  0.0 184.9 jit_solution(11464506420218188663)
XLA Ops:
  0.0 1.5 copy.12.ids_ref
  1.5 130.8 %shard_map.64 = (bf16[1024,4096]{1,0:T(8,128)(2,1)}, bf16[4,32,1024]{2,1,0:T(8,128)(2,1)}, bf16[3,128,1024]{2,1,0:T(8,128)(2,1)}, f32[16,128,128]{2,1,0:T(8,128)}) custom-call(bf16[512,1024]{1,0:T(8,128)(2,1)} %bitcast.55, bf16[3,1024,1024]{2,1,0:T(8,128)(2,1)} %w_ref.1, bf16[1024,1024]{1,0:T(8,128)(2,1)} %o_ref.1, s32[512,1]{1,0:T(8,128)} %copy.12.ids_ref, ...), custom_call_target="tpu_custom_call" | custom-call | tf_op jit(solution)/shard_map/pallas_call | solution.py:404
  132.3 0.0 copy-start
  132.3 1.2 slice_bitcast_fusion.3
  133.7 0.7 fusion.6
  134.4 1.9 %convolution_bitcast_fusion = f32[2,4,32,8,128]{4,2,1,0,3:T(8,128)S(1)} fusion(f32[2,8,128,128,1]{3,2,1,0,4:T(8,128)} %bitcast.56, bf16[4,32,8,128,1]{3,2,1,0,4:T(8,128)(2,1)S(1)} %bitcast_bitcast_fusion), kind=kOutput, calls=%fused_computation.3 | convolution fusion | flops 402653184 | bytes 2359296 | tf_op jit(solution)/shard_map/trhd,phde->ptrhe/dot_general | solution.py:550
  136.3 0.0 copy-done
  136.3 0.1 dynamic-slice_compare_fusion
  136.4 0.4 multiply_reduce_fusion
  136.9 5.7 %fusion.2.t_ref = bf16[4,32,4096]{2,1,0:T(8,128)(2,1)} fusion(bf16[1024,4096]{1,0:T(8,128)(2,1)} %get-tuple-element.11, f32[4,32,8,128]{3,1,0,2:T(8,128)S(1)} %get-tuple-element.14, f32[4,32,8]{1,0,2:T(4,128)S(1)} %add_rsqrt_fusion), kind=kOutput, calls=%fused_computation.2 | convolution fusion | flops 1074528256 | bytes 9965568 | tf_op jit(solution)/shard_map/trd,de->tre/dot_general | solution.py:557
  142.6 40.6 %shard_map.65 = bf16[4,32,1024]{2,1,0:T(8,128)(2,1)} custom-call(bf16[4,32,4096]{2,1,0:T(8,128)(2,1)} %fusion.2.t_ref, bf16[4,32,1024]{2,1,0:T(8,128)(2,1)} %get-tuple-element.12.em_ref), custom_call_target="tpu_custom_call" | custom-call | tf_op jit(solution)/shard_map/pallas_call | solution.py:514
  183.2 1.7 copy.51
  (6 shorter events, 0.2 us)
Async XLA Ops:
  132.3 4.0 %copy-start = (s32[128]{0:T(128)S(1)}, s32[128]{0:T(128)}, u32[]{:S(2)}) copy-start(s32[128]{0:T(128)} %param.11) | copy-start | bytes 1540

commit v4 on v3

--- a/solution.py
+++ b/solution.py
@@ -8,7 +8,7 @@
 from jax.sharding import PartitionSpec as P
 
 DH = 128
-SUB = 2
+SUB = 4
 MESH = pl.DeviceIdType.MESH
 
 
@@ -38,7 +38,7 @@
 
 def gather_kernel(sizes, p_ref, w_ref, o_ref, ids_ref, table_ref, of_ref, em_ref, qkv_ref, state_ref,
                   xa, wf_ref, ef_ref, acc, found, looked_ref, t_tile, t_sem, s_mine, s_chip, s_half, s_mate, s_far, s_back,
-                  s_send, s_recv, e_in, own_sem, e_send, e_recv, z_send, z_recv, x_send, x_recv,
+                  s_send, s_recv, e_in, e_out, own_sem, e_send, e_recv, z_send, z_recv, x_send, x_recv,
                   y_send, y_recv, pown_send, pown_recv, px_send, px_recv, py_send, py_recv):
     grp_n, ctx_n, head_n = sizes
     chips = ctx_n // 2
@@ -112,7 +112,7 @@
             if chips > 1:
                 start_if(x_next[way], x_copy(chunk_src(index, grp), index, way, 1, ctx))
 
-    for index in range(2):
+    for index in range(SUB):
         x_first(index)
 
     mate = chip * 2 + 1 - core
@@ -168,21 +168,41 @@
 
     def embed_send():
         looked_ref[...] = found[...].astype(looked_ref.dtype).reshape(looked_ref.shape)
-        for step in range(1, ctx_n):
-            to = lax.rem(ctx + step, ctx_n)
-            copy = remote(
-                looked_ref.at[:, pl.ds(pl.multiple_of(to * resp, resp), resp), :], e_in.at[step - 1],
-                e_send.at[step - 1], e_recv.at[step - 1], {"ctx": to},
-            )
+        for to in range(chips):
+            copy = near_copy(to)
             copy.start()
             at_end(None, copy.wait_send)
-        x_first(2)
+
+    def resp_at(owner):
+        return pl.ds(pl.multiple_of(owner * resp, resp), resp)
+
+    def near_copy(to):
+        return remote(looked_ref.at[:, resp_at(to * 2 + 1 - core), :], e_in.at[to],
+                      e_send.at[to], e_recv.at[to], partner)
+
+    def far_rows(step):
+        to = lax.rem(chip + step, chips)
+        return remote(e_out.at[step - 1], e_in.at[chips + step - 1], e_send.at[chips + step - 1],
+                      e_recv.at[chips + step - 1], {"ctx": to * 2 + core})
+
+    def near_sum(to):
+        near_copy(to).wait_recv()
+        return looked_ref[:, resp_at(to * 2 + core), :].astype(jnp.float32) + e_in[to].astype(jnp.float32)
+
+    def embed_mid():
+        for step in range(1, chips):
+            e_out[step - 1] = near_sum(lax.rem(chip + step, chips)).astype(e_out.dtype)
+            copy = far_rows(step)
+            copy.start()
+            at_end(None, copy.wait_send)
+        for index in range(SUB, 2 * SUB - 1):
+            x_first(index)
 
     def embed_sum():
-        total = looked_ref[:, pl.ds(pl.multiple_of(ctx * resp, resp), resp), :].astype(jnp.float32)
-        for step in range(1, ctx_n):
-            remote(e_in.at[step - 1], e_in.at[step - 1], e_send.at[step - 1], e_recv.at[step - 1], partner).wait_recv()
-            total += e_in[step - 1].astype(jnp.float32)
+        total = near_sum(chip)
+        for step in range(1, chips):
+            far_rows(step).wait_recv()
+            total += e_in[chips + step - 1].astype(jnp.float32)
         em_ref[...] = total.astype(em_ref.dtype)
         local = pltpu.make_async_copy(em_ref, embed_at(head), own_sem.at[3])
         local.start()
@@ -221,8 +241,8 @@
         from_chip = chip - dist if way == 0 else chip + dist
         have = from_chip >= 0 if way == 0 else from_chip < chips
         place = chunk_dst(index, from_chip * 2 + core, grp)
-        if way == 0 and dist == 1 and 1 <= index < len(chunks) - 2:
-            x_first(index + 2)
+        if way == 0 and dist == 1 and SUB - 1 <= index < len(chunks) - SUB:
+            x_first(index + SUB)
 
         @pl.when(have)
         def _():
@@ -345,21 +365,24 @@
         to_mate(s_back.at[0], s_back.at[1], 1).wait_recv()
         state_ref[theirs] = s_back[1].astype(jnp.float32)
 
+    unit = 22.0 / SUB
+
     def reach(chunk):
-        return 11.0 * (chunk + 1) + 88.0 * max(chips - 2, 0) + 12.5
-
-    middle = n_tiles // 2
-    events.append((0.0, functools.partial(lookup, 0, middle)))
-    events.append((11.5, functools.partial(lookup, middle, n_tiles)))
-    events.append((11.6, embed_send))
+        return unit * (chunk + 2) + 88.0 * max(chips - 2, 0) + 1.5
+
+    for part in range(4):
+        events.append((unit * part + 0.1 if part else 0.0,
+                       functools.partial(lookup, n_tiles * part // 4, n_tiles * (part + 1) // 4)))
+    events.append((unit * 3 + 0.2, embed_send))
+    events.append((unit * 3 + 0.3, embed_mid))
     events.append((30.0, embed_sum))
     for dist in range(1, chips):
         for index in range(len(chunks)):
-            when = 11.0 * (index + 1) + 88.0 * (dist - 1)
+            when = unit * (index + 1) + 88.0 * (dist - 1)
             for way in range(2):
                 events.append((when, functools.partial(x_event, index, way, dist)))
                 for step in range(1, grp_n):
-                    events.append((when + 12.0, functools.partial(y_event, index, way, dist, step)))
+                    events.append((when + unit + 1.0, functools.partial(y_event, index, way, dist, step)))
     ready = reach(2 * SUB - 1)
     after = ready
     for dist in range(head_n):
@@ -418,7 +441,7 @@
             pltpu.VMEM((2, p_rows, cols), jnp.float32),
             pltpu.VMEM((steps * resp_all, width), jnp.float32),
             pltpu.VMEM((steps, resp_all, width), dtype),
-            pltpu.VMEM((2, min(512, embed_table.shape[0] // 2), width), dtype),
+            pltpu.VMEM((2, min(512, embed_table.shape[0] // 4), width), dtype),
             pltpu.SemaphoreType.DMA((2,)),
             pltpu.VMEM((2 * heads, DH, DH), dtype),
             pltpu.VMEM((2 * heads, DH, DH), jnp.float32),
@@ -428,6 +451,7 @@
             pltpu.VMEM((2, heads, DH, DH), dtype),
             s_sem, s_sem,
             pltpu.VMEM((ctx_n - 1, steps, resp, width), dtype),
+            pltpu.VMEM((far, steps, resp, width), dtype),
             pltpu.SemaphoreType.DMA((4,)),
             pltpu.SemaphoreType.DMA((ctx_n - 1,)),
             pltpu.SemaphoreType.DMA((ctx_n - 1,)),
@@ -441,16 +465,22 @@
     )(prompt_hidden, qkv_weight, out_weight, response_ids.reshape(-1, 1), embed_table)
 
 
-def finish_kernel(head_n, t_ref, em_ref, out_ref, mixed, sums, parts, squares, far_squares,
-                  t_send, t_recv, q_send, q_recv):
+def finish_kernel(head_n, h_ref, of_ref, em_ref, out_ref, weights, w_sem, fresh, mixed, sums, parts,
+                  squares, far_squares, t_send, t_recv, q_send, q_recv):
     head = lax.axis_index("head")
-    width = em_ref.shape[2]
-    greet((("head", head_n),))
-    go = (head + 1 < head_n, head > 0)
+    rows, width = em_ref.shape
     have = (head > 0, head + 1 < head_n)
 
-    def term_copy(src, way, to):
-        return remote(src, parts.at[way, to], t_send.at[way, to], t_recv.at[way, to],
+    def weight_copy(to):
+        start = pl.multiple_of(to * width, width)
+        return pltpu.make_async_copy(of_ref.at[:, pl.ds(start, width)], weights.at[to], w_sem.at[to])
+
+    def product(to):
+        weight_copy(to).wait()
+        return jnp.dot(h_ref[...], weights[to], preferred_element_type=jnp.float32)
+
+    def term_copy(way, to):
+        return remote(sums.at[way, to], parts.at[way, to], t_send.at[way, to], t_recv.at[way, to],
                       {"head": head + (1 if way == 0 else -1)})
 
     def square_copy(step):
@@ -461,52 +491,53 @@
     order = []
     for step in range(head_n - 1):
         order += [(0, head_n - 1 - step), (1, step)]
+
+    def ahead(way, to):
+        return to > head if way == 0 else to < head
+
     for way, to in order:
-        ahead = to > head if way == 0 else to < head
-        own = t_ref.at[:, :, pl.ds(to * width, width)]
-
-        @pl.when(ahead & have[way])
+        pl.when(ahead(way, to))(weight_copy(to).start)
+    weight_copy(head).start()
+    greet((("head", head_n),))
+    for way, to in order:
+        @pl.when(ahead(way, to))
         def _():
-            term_copy(sums.at[way, to], way, to).wait_recv()
-            total = own[...].astype(jnp.float32) + parts[way, to].astype(jnp.float32)
-            sums[way, to] = total.astype(sums.dtype)
-            term_copy(sums.at[way, to], way, to).start()
-
-        @pl.when(ahead & jnp.logical_not(have[way]))
-        def _():
-            term_copy(own, way, to).start()
-
-    mixed[...] = em_ref[...].astype(jnp.float32) + t_ref[
-        :, :, pl.ds(pl.multiple_of(head * width, width), width)
-    ].astype(jnp.float32)
+            fresh[...] = product(to)
+
+            @pl.when(have[way])
+            def _():
+                term_copy(way, to).wait_recv()
+                fresh[...] += parts[way, to].astype(jnp.float32)
+
+            sums[way, to] = fresh[...].astype(sums.dtype)
+            term_copy(way, to).start()
+
+    mixed[...] = em_ref[...].astype(jnp.float32) + product(head)
     for way in range(2):
         @pl.when(have[way])
         def _():
-            term_copy(sums.at[way, 0], way, head).wait_recv()
+            term_copy(way, head).wait_recv()
             mixed[...] += parts[way, head].astype(jnp.float32)
 
     values = mixed[...]
-    total = jnp.broadcast_to(jnp.sum(values * values, axis=-1, keepdims=True), squares.shape)
+    total = jnp.sum(values * values, axis=-1, keepdims=True)
+    total = jnp.broadcast_to(total, (rows, 128)).T[:8]
     squares[...] = total
     for step in range(1, head_n):
         square_copy(step).start()
     for step in range(1, head_n):
         square_copy(step).wait_recv()
         total += far_squares[step - 1]
-    scale = lax.rsqrt(total[:, :, :1] / (width * head_n) + 1e-06)
-    out_ref[...] = (values * scale).astype(out_ref.dtype)
+    total = jnp.broadcast_to(total[:1], (128, rows)).T[:, :1]
+    out_ref[...] = (values * lax.rsqrt(total / (width * head_n) + 1e-06)).astype(out_ref.dtype)
     for way, to in order:
-        ahead = to > head if way == 0 else to < head
-
-        @pl.when(ahead)
-        def _():
-            term_copy(sums.at[way, to], way, to).wait_send()
+        pl.when(ahead(way, to))(term_copy(way, to).wait_send)
     for step in range(1, head_n):
         square_copy(step).wait_send()
 
 
-def finish(head_n, terms, embedded_mine):
-    steps, resp, width = embedded_mine.shape
+def finish(head_n, head_out, full_out, embedded_mine):
+    rows, width = embedded_mine.shape
     vmem = pl.BlockSpec(memory_space=pltpu.VMEM)
     others = max(head_n - 1, 1)
     sem = pltpu.SemaphoreType.DMA((others,))
@@ -514,18 +545,21 @@
     return pl.pallas_call(
         functools.partial(finish_kernel, head_n),
         out_shape=jax.ShapeDtypeStruct(embedded_mine.shape, jnp.bfloat16),
-        in_specs=[vmem, vmem],
+        in_specs=[vmem, pl.BlockSpec(memory_space=pl.ANY), vmem],
         out_specs=vmem,
         scratch_shapes=[
-            pltpu.VMEM(embedded_mine.shape, jnp.float32),
-            pltpu.VMEM((2, head_n) + embedded_mine.shape, jnp.bfloat16),
-            pltpu.VMEM((2, head_n) + embedded_mine.shape, jnp.bfloat16),
-            pltpu.VMEM((steps, resp, 128), jnp.float32),
-            pltpu.VMEM((others, steps, resp, 128), jnp.float32),
+            pltpu.VMEM((head_n, full_out.shape[0], width), jnp.bfloat16),
+            pltpu.SemaphoreType.DMA((head_n,)),
+            pltpu.VMEM((rows, width), jnp.float32),
+            pltpu.VMEM((rows, width), jnp.float32),
+            pltpu.VMEM((2, head_n, rows, width), jnp.bfloat16),
+            pltpu.VMEM((2, head_n, rows, width), jnp.bfloat16),
+            pltpu.VMEM((8, rows), jnp.float32),
+            pltpu.VMEM((others, 8, rows), jnp.float32),
             t_sem, t_sem, sem, sem,
         ],
         compiler_params=pltpu.CompilerParams(collective_id=1, has_side_effects=True),
-    )(terms, embedded_mine)
+    )(head_out, full_out, embedded_mine)
 
 
 def on_device(sizes, prompt_hidden, qkv_weight, out_weight, embed_table, response_ids, assignment):
@@ -553,9 +587,11 @@
     later = jnp.arange(steps)[:, None] >= jnp.arange(steps)[None, :]
     scores = jnp.where(later[None, None], scores, 0.0).astype(jnp.bfloat16)
     local = jnp.einsum("rhts,srhd->trhd", scores, value, preferred_element_type=jnp.float32)
-    head_out = rms_rows(chosen + local).astype(jnp.bfloat16).reshape(steps, resp_local, local_cols)
-    terms = jnp.einsum("trd,de->tre", head_out, full_out, preferred_element_type=jnp.float32)
-    return finish(sizes[2], terms.astype(jnp.bfloat16), embedded_mine)
+    head_out = rms_rows(chosen + local).astype(jnp.bfloat16).reshape(steps * resp_local, local_cols)
+    result = finish(
+        sizes[2], head_out, full_out, embedded_mine.reshape(steps * resp_local, local_cols)
+    )
+    return result.reshape(steps, resp_local, local_cols)
 
 
 def solution(mesh):

time: 185 us -> 178 us (0.962)
  matrix products: 8.34 us -> 2.6 us
  Pallas kernels: 171 us -> 169 us
    dot_general x1 -> x0, matrix products: 5.75 us -> none  [on_device(): jnp.einsum('trd,de->tre', head_out, full_out, preferred_element_type=jnp....]
    pallas_call x1, Pallas kernels: 40.6 us -> 38.3 us  [finish(): pl.pallas_call(functools.partial(finish_kernel, head_n), out_shape=jax.Sh...]
    unnamed x7 -> x8, local copies, waits for them, and re-layouts: 2.98 us -> 3.73 us
where the time goes in v4:
time: 178 us
  Pallas kernels  169 us (95%)
  local copies, waits for them, and re-layouts  5.46 us (3%)
  matrix products  2.6 us (1%)
    pallas_call x1, Pallas kernels, gather_all(): pl.pallas_call(functools.partial(gather_kernel, sizes), out_shape=(jax.Sh...  131 us
    pallas_call x1, Pallas kernels, finish(): pl.pallas_call(functools.partial(finish_kernel, head_n), out_shape=jax.Sh...  38.3 us
    unnamed x8, local copies, waits for them, and re-layouts  3.73 us

profile of v4, /device:TPU:0, one launch (start us, length us, event | category | flops | bytes accessed | tf_op | source)
XLA Modules:
  0.0 177.9 jit_solution(12149396815325154559)
XLA Ops:
  0.0 1.5 copy.13.ids_ref
  1.5 130.8 %shard_map.64 = (bf16[1024,4096]{1,0:T(8,128)(2,1)}, bf16[4,32,1024]{2,1,0:T(8,128)(2,1)}, bf16[3,128,1024]{2,1,0:T(8,128)(2,1)}, f32[16,128,128]{2,1,0:T(8,128)}) custom-call(bf16[512,1024]{1,0:T(8,128)(2,1)} %bitcast.50, bf16[3,1024,1024]{2,1,0:T(8,128)(2,1)} %w_ref.1, bf16[1024,1024]{1,0:T(8,128)(2,1)} %o_ref.1, s32[512,1]{1,0:T(8,128)} %copy.13.ids_ref, ...), custom_call_target="tpu_custom_call" | custom-call | tf_op jit(solution)/shard_map/pallas_call | solution.py:427
  132.3 0.0 copy-start
  132.3 1.2 slice_bitcast_fusion.3
  133.7 0.7 fusion.1
  134.4 1.9 %convolution_bitcast_fusion = f32[2,4,32,8,128]{4,2,1,0,3:T(8,128)S(1)} fusion(f32[2,8,128,128,1]{3,2,1,0,4:T(8,128)} %bitcast.53, bf16[4,32,8,128,1]{3,2,1,0,4:T(8,128)(2,1)S(1)} %bitcast_bitcast_fusion), kind=kOutput, calls=%fused_computation | convolution fusion | flops 402653184 | bytes 2359296 | tf_op jit(solution)/shard_map/trhd,phde->ptrhe/dot_general | solution.py:584
  136.3 0.0 copy-done
  136.3 0.1 dynamic-slice_compare_fusion
  136.4 0.4 multiply_reduce_fusion
  136.8 0.2 multiply_convert_fusion
  137.0 0.2 copy.19
  137.2 0.8 copy.48
  138.0 38.3 %shard_map.65 = bf16[128,1024]{1,0:T(8,128)(2,1)} custom-call(bf16[128,1024]{1,0:T(8,128)(2,1)} %bitcast.51, bf16[1024,4096]{1,0:T(8,128)(2,1)} %get-tuple-element.11.of_ref, bf16[128,1024]{1,0:T(8,128)(2,1)} %bitcast.57), custom_call_target="tpu_custom_call" | custom-call | tf_op jit(solution)/shard_map/pallas_call | solution.py:545
  176.2 1.7 copy.50
  (6 shorter events, 0.2 us)
Async XLA Ops:
  132.3 4.0 %copy-start = (s32[128]{0:T(128)S(1)}, s32[128]{0:T(128)}, u32[]{:S(2)}) copy-start(s32[128]{0:T(128)} %param.11) | copy-start | bytes 1540

commit v5 on v4

--- a/solution.py
+++ b/solution.py
@@ -226,7 +226,7 @@
     for dist in range(1, head_n):
         for way in range(2):
             events.append((22.0 * dist, functools.partial(z_event, 0, way, dist)))
-            events.append((22.0 * dist + 20.0, functools.partial(z_event, 1, way, dist)))
+            events.append((22.0 * dist + 14.0, functools.partial(z_event, 1, way, dist)))
 
     def pass_on(ok, dst, send, recv):
         copy = remote(dst, dst, send, recv, partner)
@@ -391,6 +391,7 @@
     embedded_at = 22.0 * (head_n - 1) + 20.5
     events.append((after + 0.1, make_state))
     events.append((after + 0.2, chip_state))
+    embedded_at -= 6.0
     after = max(after + 0.3, embedded_at)
     events.append((after, norm_rows))
     events.append((after + 0.2, functools.partial(project, 1)))

time: 178 us -> 186 us (1.045)
  Pallas kernels: 169 us -> 176 us
    pallas_call x1, Pallas kernels: 38.3 us -> 41.8 us  [finish(): pl.pallas_call(functools.partial(finish_kernel, head_n), out_shape=jax.Sh...]
    pallas_call x1, Pallas kernels: 131 us -> 134 us  [gather_all(): pl.pallas_call(functools.partial(gather_kernel, sizes), out_shape=(jax.Sh...]
where the time goes in v5:
time: 186 us; the launch traced here: 185 us
  Pallas kernels  176 us (95%)
  local copies, waits for them, and re-layouts  5.46 us (3%)
  matrix products  2.6 us (1%)
    pallas_call x1, Pallas kernels, gather_all(): pl.pallas_call(functools.partial(gather_kernel, sizes), out_shape=(jax.Sh...  134 us
    pallas_call x1, Pallas kernels, finish(): pl.pallas_call(functools.partial(finish_kernel, head_n), out_shape=jax.Sh...  41.8 us
    unnamed x8, local copies, waits for them, and re-layouts  3.73 us

profile of v5, /device:TPU:0, one launch (start us, length us, event | category | flops | bytes accessed | tf_op | source)
XLA Modules:
  0.0 185.0 jit_solution(8419542059731982711)
XLA Ops:
  0.0 1.5 copy.13.ids_ref
  1.5 134.3 %shard_map.64 = (bf16[1024,4096]{1,0:T(8,128)(2,1)}, bf16[4,32,1024]{2,1,0:T(8,128)(2,1)}, bf16[3,128,1024]{2,1,0:T(8,128)(2,1)}, f32[16,128,128]{2,1,0:T(8,128)}) custom-call(bf16[512,1024]{1,0:T(8,128)(2,1)} %bitcast.50, bf16[3,1024,1024]{2,1,0:T(8,128)(2,1)} %w_ref.1, bf16[1024,1024]{1,0:T(8,128)(2,1)} %o_ref.1, s32[512,1]{1,0:T(8,128)} %copy.13.ids_ref, ...), custom_call_target="tpu_custom_call" | custom-call | tf_op jit(solution)/shard_map/pallas_call | solution.py:428
  135.9 0.0 copy-start
  135.9 1.2 slice_bitcast_fusion.3
  137.2 0.7 fusion.1
  138.0 1.9 %convolution_bitcast_fusion = f32[2,4,32,8,128]{4,2,1,0,3:T(8,128)S(1)} fusion(f32[2,8,128,128,1]{3,2,1,0,4:T(8,128)} %bitcast.53, bf16[4,32,8,128,1]{3,2,1,0,4:T(8,128)(2,1)S(1)} %bitcast_bitcast_fusion), kind=kOutput, calls=%fused_computation | convolution fusion | flops 402653184 | bytes 2359296 | tf_op jit(solution)/shard_map/trhd,phde->ptrhe/dot_general | solution.py:585
  139.9 0.0 copy-done
  139.9 0.1 dynamic-slice_compare_fusion
  139.9 0.4 multiply_reduce_fusion
  140.4 0.2 multiply_convert_fusion
  140.6 0.2 copy.19
  140.8 0.8 copy.48
  141.5 41.8 %shard_map.65 = bf16[128,1024]{1,0:T(8,128)(2,1)} custom-call(bf16[128,1024]{1,0:T(8,128)(2,1)} %bitcast.51, bf16[1024,4096]{1,0:T(8,128)(2,1)} %get-tuple-element.11.of_ref, bf16[128,1024]{1,0:T(8,128)(2,1)} %bitcast.57), custom_call_target="tpu_custom_call" | custom-call | tf_op jit(solution)/shard_map/pallas_call | solution.py:546
  183.4 1.7 copy.50
  (6 shorter events, 0.2 us)
Async XLA Ops:
  135.9 4.0 %copy-start = (s32[128]{0:T(128)S(1)}, s32[128]{0:T(128)}, u32[]{:S(2)}) copy-start(s32[128]{0:T(128)} %param.11) | copy-start | bytes 1540
